TPU v7x, 128 devices: a whole 4x4x4 slice. The times are simulated.
128 devices in a mesh: expert: 8 (over y, core), row: 16 (over x, z).
Axes of the slice: x: 4, y: 4, z: 4, core: 2. Of those that a mesh axis runs over, the one named last changes fastest.
Arguments:
- sampled: int32 [8, 32], P('expert'), may hold values from 0 to 31, each once within a row
- refresh: int32 [256], P('expert'), may hold values 0 or 1
- momentum_bank: bfloat16 [256, 2048, 512], P('expert', 'row'), may hold values from -6 to 6
- weights: bfloat16 [256, 2048, 512], P('expert', 'row'), may hold values from -6 to 6
- grads: bfloat16 [256, 2048, 512], P('expert', 'row'), may hold values from -6 to 6
- basis: float32 [256, 2048, 64], P('expert', 'row'), may hold values from -0.125 to 0.125
Outputs:
- new_bank: bfloat16 [256, 2048, 512], P('expert', 'row')
- new_weights: bfloat16 [256, 2048, 512], P('expert', 'row')
Inputs may be any that keep to these rules, and one draw needn't show every extreme that they name: Each row of sampled names every number of 0 to 31 once.
All inputs are finite; a program needn't handle non-finite values. No bound on the sum of `refresh` on one device may be relied on, other than what follows from the above.
Results may differ from a plain program's by a relative error of at most 0.0045.
Values may be sent and summed in bfloat16 or wider, within the bound.
No kernel may reach another device: no remote copies, remote signals or barrier semaphores. Data moves between devices by JAX's collectives and lax.ppermute only.
A program may use at most 128 MiB of HBM per device.

v0:
```python
import math

import jax
import jax.numpy as jnp
from jax import lax
from jax.sharding import PartitionSpec as P

D = 2048
FF = 512
ITERS = 3


momentum_decay = 0.9
residual_weight = 2.0
step_rate = 0.5
decay_rate = 0.1
coef_first = 3.4445
coef_second = -4.775
coef_third = 2.0315
epsilon = 1e-07


def cut_along(array, dim, length):
    shape = array.shape
    parts = array.reshape(*shape[:dim], length, shape[dim] // length, *shape[dim + 1 :])
    return jnp.moveaxis(parts, dim, 0)


def cut_rows(length, count):
    lap = length // count
    if lap >= 8:
        lap -= lap % 8
    return [lap * k for k in range(1, count)]


def joined_along(parts, dim):
    shape = list(parts.shape[1:])
    shape[dim] *= parts.shape[0]
    return jnp.moveaxis(parts, 0, dim).reshape(shape)


def exchange_in_pieces(array, axis, pieces, split_dim, concat_dim):
    parts = cut_along(array, split_dim, lax.axis_size(axis))
    cut = max(range(1, max(2, parts.ndim - 1)), key=lambda d: parts.shape[d])
    gathered = []
    for slab in jnp.split(parts, cut_rows(parts.shape[cut], pieces), axis=cut):
        if slab.size:
            gathered.append(lax.all_to_all(slab, axis, split_axis=0, concat_axis=0, tiled=True))
    return joined_along(jnp.concatenate(gathered, axis=cut), concat_dim)


def orthogonalize(block):
    matrices = block[0]
    values = matrices.astype(jnp.float32)
    total_norm = jnp.sqrt(jnp.sum(values * values, axis=(1, 2), keepdims=True)) + epsilon
    iterate = (values / total_norm).astype(jnp.bfloat16)
    for sweep in range(ITERS):
        gram = jnp.einsum(
            "mdi,mdj->mij", iterate, iterate, preferred_element_type=jnp.float32
        ).astype(jnp.bfloat16)
        square = jnp.einsum("mij,mjk->mik", gram, gram, preferred_element_type=jnp.float32)
        gram_full = lax.optimization_barrier(gram).astype(jnp.float32)
        poly = (coef_second * gram_full + coef_third * square).astype(jnp.bfloat16)
        product = jnp.einsum("mdi,mij->mdj", iterate, poly, preferred_element_type=jnp.float32)
        iterate = (coef_first * iterate.astype(jnp.float32) + product).astype(jnp.bfloat16)
    return iterate[None]


def shards(sampled, refresh, momentum_bank, weights, grads, basis):
    group_count = weights.shape[0]
    chosen = sampled[0, :group_count]
    old = momentum_bank[chosen].astype(jnp.float32)
    basis_high = basis.astype(jnp.bfloat16)
    basis_low = (basis - basis_high.astype(jnp.float32)).astype(jnp.bfloat16)
    partial_sum = jnp.einsum("srk,srf->skf", basis_high, grads, preferred_element_type=jnp.float32)
    partial_sum = partial_sum + jnp.einsum(
        "srk,srf->skf", basis_low, grads, preferred_element_type=jnp.float32
    )
    proj = lax.psum(partial_sum.astype(jnp.bfloat16), "row").astype(jnp.float32)
    low = jnp.einsum("srk,skf->srf", basis, proj, precision=lax.Precision.HIGH)
    weight_flag = refresh.astype(jnp.float32)[:, None, None]
    grad_full = grads.astype(jnp.float32)
    mom = (momentum_decay * old + low + residual_weight * weight_flag * (grad_full - low)).astype(
        jnp.bfloat16
    )
    new_bank = momentum_bank.at[chosen].set(mom)
    owners = lax.axis_size("row")
    row_count = weights.shape[1]
    per_owner = weights.shape[0] // owners
    packed = mom.reshape(owners, per_owner, row_count, weights.shape[2])
    gathered = exchange_in_pieces(packed, "row", 2, 0, 2)
    result = orthogonalize(gathered)
    returned = lax.all_to_all(result, "row", split_axis=2, concat_axis=0, tiled=True)
    ortho = returned.reshape(weights.shape)
    scale_step = step_rate * 0.2 * math.sqrt(max(D, FF))
    updated = weights.astype(jnp.float32) * (
        1.0 - step_rate * decay_rate
    ) - scale_step * ortho.astype(jnp.float32)
    return (new_bank, updated.astype(jnp.bfloat16))


def solution(mesh):
    in_specs = (
        P("expert", None),
        P("expert"),
        P("expert", "row", None),
        P("expert", "row", None),
        P("expert", "row", None),
        P("expert", "row", None),
    )
    out_specs = (P("expert", "row", None), P("expert", "row", None))
    return jax.shard_map(shards, mesh=mesh, in_specs=in_specs, out_specs=out_specs, check_vma=False)
```

profile of v0, /device:TPU:64, one launch (start us, length us, event | category | flops | bytes accessed | tf_op | source)
XLA Modules:
  0.0 308.1 jit_solution(14402531057384266244)
XLA Ops:
  7.2 0.0 all-reduce.2.cloned.1.call-start
  7.2 0.0 copy-start.1
  7.2 4.8 %copy.27 = bf16[32,128,512]{2,1,0:T(8,128)(2,1)} copy(bf16[32,128,512]{2,1,0:T(8,128)(2,1)} %param.8) | data formatting | bytes 8388608
  12.0 0.7 fusion.7
  12.8 2.2 add_convert_fusion.3
  14.9 0.0 all-reduce.2.cloned.1.call-update
  15.0 5.0 %gather_fusion = bf16[32,128,512]{2,1,0:T(8,128)(2,1)} fusion(bf16[32,128,512]{2,1,0:T(8,128)(2,1)} %copy.27, s32[1024]{0:T(1024)S(1)} %pad_clamp_fusion), kind=kCustom, calls=%fused_computation | custom fusion | bytes 8388736 | tf_op jit(solution)/shard_map/gather | solution.py:72
  20.0 86.3 %all-reduce.2.cloned.1.call-done = bf16[32,64,512]{2,1,0:T(8,128)(2,1)} async-done(((bf16[32,64,512]{2,1,0:T(8,128)(2,1)}), bf16[32,64,512]{2,1,0:T(8,128)(2,1)}) %all-reduce.2.cloned.1.call-update) | async-done | bytes 2097168 | tf_op jit(solution)/shard_map/psum | solution.py:79
  106.3 8.3 %fusion.3 = bf16[32,128,512]{2,1,0:T(8,128)(2,1)S(1)} fusion(bf16[32,128,512]{2,1,0:T(8,128)(2,1)} %param.10, bf16[32,128,512]{2,1,0:T(8,128)(2,1)} %gather_fusion, f32[32]{0:T(128)S(1)} %convert_multiply_fusion.2, bf16[32,64,512]{2,1,0:T(8,128)(2,1)} %all-reduce.2.cloned.1.call-done, f32[32,128,64]{1,2,0:T(8,128)S(1)} %copy-done.4), kind=kOutput, calls=%fused_computation.10 | convolution fusion | flops 822083584 | bytes 15728768 | tf_op jit(solution)/shard_map/srk,skf->srf/dot_general | solution.py:80
  114.6 0.3 fusion.16
  114.9 1.7 copy-done
  116.6 30.9 %all_to_all.19 = bf16[16,1,2,64,512]{4,3,2,1,0:T(8,128)(2,1)S(1)} all-to-all(bf16[16,1,2,64,512]{4,3,2,1,0:T(8,128)(2,1)S(1)} %get-tuple-element.2), channel_id=1, replica_groups=mesh['expert'=8,'row'=16] {'row'}, dimensions={0} | all-to-all | bytes 4194304 | tf_op jit(solution)/shard_map/all_to_all | solution.py:48
  147.5 28.5 %all_to_all.20 = bf16[16,1,2,64,512]{4,3,2,1,0:T(8,128)(2,1)S(1)} all-to-all(bf16[16,1,2,64,512]{4,3,2,1,0:T(8,128)(2,1)S(1)} %get-tuple-element.3), channel_id=1, replica_groups=mesh['expert'=8,'row'=16] {'row'}, dimensions={0} | all-to-all | bytes 4194304 | tf_op jit(solution)/shard_map/all_to_all | solution.py:48
  176.0 2.3 fusion
  178.4 1.2 convert_bitcast_fusion
  179.6 1.6 copy.15
  181.2 1.3 divide_convert_fusion
  182.5 2.0 copy-done.2
  184.5 2.4 convolution_convert_fusion.2
  186.9 7.6 %add_convert_fusion.2 = bf16[2,2048,512]{2,1,0:T(8,128)(2,1)} fusion(bf16[2,2048,512]{2,1,0:T(8,128)(2,1)} %copy-done.2, bf16[2,512,512]{2,1,0:T(8,128)(2,1)S(1)} %convolution_convert_fusion.2), kind=kOutput, calls=%fused_computation.15 | convolution fusion | flops 2695364608 | bytes 9437184 | tf_op jit(solution)/shard_map/mdi,mij->mdj/dot_general | solution.py:64
  194.5 5.8 %convolution_convert_fusion.1 = bf16[2,512,512]{2,1,0:T(8,128)(2,1)S(1)} fusion(bf16[2,2048,512]{2,1,0:T(8,128)(2,1)} %add_convert_fusion.2), kind=kOutput, calls=%fused_computation.24 | convolution fusion | flops 2148007936 | bytes 5242880 | tf_op jit(solution)/shard_map/mdi,mdj->mij/dot_general | solution.py:58
  200.3 7.6 %add_convert_fusion.1 = bf16[2,2048,512]{2,1,0:T(8,128)(2,1)} fusion(bf16[2,2048,512]{2,1,0:T(8,128)(2,1)} %add_convert_fusion.2, bf16[2,512,512]{2,1,0:T(8,128)(2,1)S(1)} %convolution_convert_fusion.1), kind=kOutput, calls=%fused_computation.14 | convolution fusion | flops 2695364608 | bytes 9437184 | tf_op jit(solution)/shard_map/mdi,mij->mdj/dot_general | solution.py:64
  207.9 5.8 %convolution_convert_fusion = bf16[2,512,512]{2,1,0:T(8,128)(2,1)S(1)} fusion(bf16[2,2048,512]{2,1,0:T(8,128)(2,1)} %add_convert_fusion.1), kind=kOutput, calls=%fused_computation.23 | convolution fusion | flops 2148007936 | bytes 5242880 | tf_op jit(solution)/shard_map/mdi,mdj->mij/dot_general | solution.py:58
  213.7 7.6 %fusion.5 = bf16[1,2,2048,512]{3,2,1,0:T(8,128)(2,1)} fusion(bf16[2,2048,512]{2,1,0:T(8,128)(2,1)} %add_convert_fusion.1, bf16[2,512,512]{2,1,0:T(8,128)(2,1)S(1)} %convolution_convert_fusion), kind=kOutput, calls=%fused_computation.17 | convolution fusion | flops 2695364608 | bytes 9437184 | tf_op jit(solution)/shard_map/mdi,mij->mdj/dot_general | solution.py:64
  221.3 10.1 %copy.19 = bf16[1,2,2048,512]{3,1,0,2:T(2,128)(2,1)} copy(bf16[1,2,2048,512]{3,2,1,0:T(8,128)(2,1)} %fusion.5) | data formatting | bytes 8388608 | tf_op jit(solution)/shard_map/broadcast_in_dim | solution.py:66
  231.4 6.7 %all-to-all-start.2 = ((bf16[1,2,2048,512]{3,1,0,2:T(2,128)(2,1)}), bf16[1,2,2048,512]{3,1,0,2:T(2,128)(2,1)}, u32[]{:S(2)}, u32[]{:S(2)}) async-start(bf16[1,2,2048,512]{3,1,0,2:T(2,128)(2,1)} %copy.19), calls=%async_computation.2 | async-start | bytes 8388608 | tf_op jit(solution)/shard_map/all_to_all | solution.py:93
  238.1 11.2 %scatter_fusion = bf16[32,128,512]{2,1,0:T(8,128)(2,1)} fusion(bf16[32,128,512]{2,1,0:T(8,128)(2,1)} %copy.27, s32[32]{0:T(128)S(1)} %fusion.9, bf16[32,128,512]{2,1,0:T(8,128)(2,1)} %copy-done), kind=kCustom, calls=%fused_computation.1 | custom fusion | bytes 12583040 | tf_op jit(solution)/shard_map/scatter | solution.py:86
  249.3 39.1 %all-to-all-done.2 = bf16[1,2,2048,512]{3,1,0,2:T(2,128)(2,1)} async-done(((bf16[1,2,2048,512]{3,1,0,2:T(2,128)(2,1)}), bf16[1,2,2048,512]{3,1,0,2:T(2,128)(2,1)}, u32[]{:S(2)}, u32[]{:S(2)}) %all-to-all-start.2) | async-done | bytes 4194336 | tf_op jit(solution)/shard_map/all_to_all | solution.py:93
  288.4 5.5 %convert_multiply_fusion.1 = f32[1,2,2048,512]{3,1,0,2:T(2,128)S(1)} fusion(bf16[1,2,2048,512]{3,1,0,2:T(2,128)(2,1)} %all-to-all-done.2), kind=kLoop, calls=%fused_computation.12 | loop fusion | flops 4194304 | bytes 12582912 | tf_op jit(solution)/shard_map/mul | solution.py:98
  294.0 1.6 copy.20
  295.5 0.6 copy-done.3
  296.1 5.1 %fusion.1 = bf16[32,128,512]{2,1,0:T(8,128)(2,1)} fusion(f32[16,1,2,128,512]{4,3,2,0,1:T(8,128)S(1)} %copy.20, bf16[32,128,512]{2,1,0:T(8,128)(2,1)S(1)} %copy-done.3), kind=kLoop, calls=%fused_computation.6 | loop fusion | flops 8388608 | bytes 16777216 | tf_op jit(solution)/shard_map/convert_element_type | solution.py:99
  (14 shorter events, 0.1 us)
Async XLA Ops:
  7.2 4.9 %copy-start.4 = (f32[32,128,64]{1,2,0:T(8,128)S(1)}, f32[32,128,64]{1,2,0:T(8,128)}, u32[]{:S(2)}) copy-start(f32[32,128,64]{1,2,0:T(8,128)} %param.11) | copy-start | bytes 3145732
  7.2 99.2 %all-reduce.2.cloned.1.call-start = ((), (), s32[]{:S(2)}) async-start(), calls=%async_computation.3 | async-start | bytes 4194304 | tf_op jit(solution)/shard_map/psum | solution.py:79
  7.2 4.8 %copy-start.1 = (bf16[32,128,512]{2,1,0:T(8,128)(2,1)S(1)}, bf16[32,128,512]{2,1,0:T(8,128)(2,1)}, u32[]{:S(2)}) copy-start(bf16[32,128,512]{2,1,0:T(8,128)(2,1)} %param.10) | copy-start | bytes 12582916
  12.7 2.2 copy-start.5
  15.0 5.0 %copy-start.6 = (s32[32]{0:T(128)S(1)}, s32[32]{0:T(128)}, u32[]{:S(2)}) copy-start(s32[32]{0:T(128)} %param.7) | copy-start | bytes 388
  114.6 2.0 copy-start
  182.5 2.0 copy-start.2
  231.4 57.0 %all-to-all-start.2 = ((bf16[1,2,2048,512]{3,1,0,2:T(2,128)(2,1)}), bf16[1,2,2048,512]{3,1,0,2:T(2,128)(2,1)}, u32[]{:S(2)}, u32[]{:S(2)}) async-start(bf16[1,2,2048,512]{3,1,0,2:T(2,128)(2,1)} %copy.19), calls=%async_computation.2 | async-start | bytes 8388608 | tf_op jit(solution)/shard_map/all_to_all | solution.py:93
  294.0 2.2 copy-start.3
Sparse Core Ops, SparseCore 0:
  15.1 91.1 all-reduce.1
where the time goes:
time: 309 us; the launch traced here: 308 us
  waiting for transfers between devices  125 us (40%)
  blocking collectives  59.4 us (19%)
  matrix products  47.9 us (16%)
  local copies, waits for them, and re-layouts  38.9 us (13%)
  other arithmetic  15.5 us (5%)
  between operations  14.2 us (5%)
  starting transfers between devices  6.72 us (2%)
    psum x1, waiting for transfers between devices, shards(): proj = lax.psum(partial_sum.astype(jnp.bfloat16), 'row').astype(jnp.float32)  86.3 us
    all_to_all x2, blocking collectives, exchange_in_pieces(): lax.all_to_all(slab, axis, split_axis=0, concat_axis=0, tiled=True)  59.4 us
    all_to_all x1, waiting for transfers between devices, shards(): lax.all_to_all(result, 'row', split_axis=2, concat_axis=0, tiled=True)  39.1 us
    dot_general x3, matrix products, orthogonalize(): jnp.einsum('mdi,mij->mdj', iterate, poly, preferred_element_type=jnp.floa...  22.7 us
    dot_general x3, matrix products, orthogonalize(): jnp.einsum('mdi,mdj->mij', iterate, iterate, preferred_element_type=jnp.f...  14 us
    scatter x1, local copies, waits for them, and re-layouts, shards(): new_bank = momentum_bank.at[chosen].set(mom)  11.2 us
    broadcast_in_dim x1, local copies, waits for them, and re-layouts, orthogonalize(): return iterate[None]  10.1 us
    unnamed x15, local copies, waits for them, and re-layouts  9.11 us
  transfers between devices with their start and end apart: 2, of which 2 were waited for; matrix products, arithmetic and copies ran while one was open for 5% of the time, Pallas kernels for 0%

commit v1 on v0

v1 whole, which is shorter than its diff:
```python
import functools
import math

import jax
import jax.numpy as jnp
from jax import lax
from jax.experimental import pallas as pl
from jax.experimental.pallas import tpu as pltpu
from jax.sharding import PartitionSpec as P

D = 2048
FF = 512
HALF = 256
RANK = 64
ROWS = 128
SIDE = 4
PER_CHUNK = 16
CHUNKS = 2
PACK = ROWS + 16
FULL = PACK + RANK
MIX = SIDE * PACK + RANK
BACK = SIDE * ROWS + RANK
LAST = SIDE * ROWS + SIDE * RANK

momentum_decay = 0.9
residual_weight = 2.0
step_rate = 0.5
decay_rate = 0.1
coef_first = 3.4445
coef_second = -4.775
coef_third = 2.0315
epsilon = 1e-07


SMEM = pl.BlockSpec(memory_space=pltpu.SMEM)
VMEM = pl.BlockSpec(memory_space=pltpu.VMEM)
HBM = pl.BlockSpec(memory_space=pltpu.HBM)
bf16 = jnp.bfloat16
f32 = jnp.float32


def shape(*dims, dtype=bf16):
    return jax.ShapeDtypeStruct(dims, dtype)


def call(kernel, out_shape, in_specs, out_specs, scratch, limit, flops, moved, aliases=None):
    return pl.pallas_call(
        kernel,
        out_shape=out_shape,
        in_specs=in_specs,
        out_specs=out_specs,
        scratch_shapes=scratch,
        input_output_aliases=aliases or {},
        compiler_params=pltpu.CompilerParams(vmem_limit_bytes=limit << 20),
        cost_estimate=pl.CostEstimate(flops=int(flops), bytes_accessed=int(moved), transcendentals=0),
    )


def position():
    me = lax.axis_index("row")
    return lax.div(me, SIDE), lax.rem(me, SIDE)


def plus(place, dx, dz):
    return lax.rem(place[0] + dx, SIDE) * SIDE + lax.rem(place[1] + dz, SIDE)


def mm(a, b):
    return jnp.dot(a, b, preferred_element_type=f32)


def mm_t(a, b):
    return lax.dot_general(a, b, (((0,), (0,)), ((), ())), preferred_element_type=f32)


def halves(value):
    high = value.astype(bf16)
    return jnp.concatenate([high, (value - high.astype(f32)).astype(bf16)], axis=0)


def added(parts):
    total = parts[0].astype(f32)
    for part in parts[1:]:
        total = total + part.astype(f32)
    return total.astype(bf16)


def pack_kernel(chunk, top, chosen_in, refresh_in, grads, bank, basis, *rest):
    left, right = rest[:SIDE], rest[SIDE : 2 * SIDE]
    g, old, bt, chosen, refresh, sems, flags = rest[2 * SIDE :]
    place = position()
    base = chunk * PER_CHUNK
    small = (
        pltpu.make_async_copy(chosen_in, chosen, flags.at[0]),
        pltpu.make_async_copy(refresh_in, refresh, flags.at[1]),
    )
    for copy in small:
        copy.start()

    def copies(i):
        s = base + plus(place, i // SIDE, i % SIDE)
        return (
            pltpu.make_async_copy(grads.at[s], g.at[i], sems.at[0, i]),
            pltpu.make_async_copy(basis.at[s], bt.at[i], sems.at[1, i]),
        )

    def old_copy(i):
        s = base + plus(place, i // SIDE, i % SIDE)
        return pltpu.make_async_copy(bank.at[chosen[0, s]], old.at[i], sems.at[2, i])

    for i in range(4):
        for copy in copies(i):
            copy.start()
    for copy in small:
        copy.wait()
    for i in range(PER_CHUNK):
        if i >= 4:
            for copy in copies(i):
                copy.start()
        old_copy(i).start()

    for i in range(PER_CHUNK):
        dx, dz = i // SIDE, i % SIDE
        if dz == 0:
            for j in range(i, i + SIDE):
                for copy in copies(j):
                    copy.wait()
                old_copy(j).wait()
        flag = residual_weight * refresh[base + plus(place, dx, dz)].astype(f32)
        both = halves(bt[i])
        for side in range(2):
            cols = slice(side * HALF, (side + 1) * HALF)
            out, at = (left[dx], dz) if side == 0 else (right[dz], dx)
            at = top + at * FULL
            grad = g[i, :, cols]
            value = momentum_decay * old[i, :, cols].astype(f32) + flag * grad.astype(f32)
            out[at : at + ROWS] = value.astype(bf16)
            first = 32 * side
            out[at + ROWS : at + PACK, :128] = both[first : first + 16]
            out[at + ROWS : at + PACK, 128:] = both[first + 16 : first + 32]
            part = mm(both, grad)
            out[at + PACK : at + FULL] = (part[:RANK] + part[RANK:]).astype(bf16)


def pack(chunk, top, chosen, refresh, grads, bank, basis):
    return call(
        functools.partial(pack_kernel, chunk, top),
        [shape(top + SIDE * FULL, HALF)] * (2 * SIDE),
        [HBM] * 5,
        [VMEM] * (2 * SIDE),
        [
            pltpu.VMEM((PER_CHUNK, ROWS, FF), bf16),
            pltpu.VMEM((PER_CHUNK, ROWS, FF), bf16),
            pltpu.VMEM((PER_CHUNK, RANK, ROWS), f32),
            pltpu.SMEM((1, CHUNKS * PER_CHUNK), jnp.int32),
            pltpu.SMEM((CHUNKS * PER_CHUNK,), jnp.int32),
            pltpu.SemaphoreType.DMA((3, PER_CHUNK)),
            pltpu.SemaphoreType.DMA((2,)),
        ],
        22,
        3e8,
        9e6,
    )(chosen, refresh, grads, bank, basis)


def mix_kernel(top, count, *refs):
    outs = refs[count:]
    for side in range(2):
        got = refs[side * SIDE : (side + 1) * SIDE]
        out = outs[side * SIDE : (side + 1) * SIDE]
        for to in range(SIDE):
            at = top + to * FULL
            for src in range(SIDE):
                out[to][src * PACK : (src + 1) * PACK] = got[src][at : at + PACK]
            out[to][SIDE * PACK : MIX] = added([ref[at + PACK : at + FULL] for ref in got])


def mix(top, got, into):
    rows = MIX if into is None else into[0].shape[0]
    into = into or []
    return call(
        functools.partial(mix_kernel, top, len(got) + len(into)),
        [shape(rows, HALF)] * (2 * SIDE),
        [VMEM] * (len(got) + len(into)),
        [VMEM] * (2 * SIDE),
        [],
        16,
        1e6,
        6e6,
        {len(got) + k: k for k in range(len(into))},
    )(*got, *into)


def ortho_kernel(chunk, top, refresh, *refs):
    q_left, q_right = refs[:SIDE], refs[SIDE : 2 * SIDE]
    b_left, b_right = refs[2 * SIDE : 3 * SIDE], refs[3 * SIDE : 4 * SIDE]
    m, acc, gram, b_one, q_mat = refs[4 * SIDE :]
    place = position()
    keep = 1.0 - residual_weight * refresh[chunk * PER_CHUNK + plus(place, 0, 0)].astype(f32)
    proj = [added([ref[SIDE * PACK : MIX] for ref in q]) for q in (q_left, q_right)]
    for k in range(SIDE):
        b_left[k][top + SIDE * ROWS : top + SIDE * ROWS + RANK] = proj[0]
        b_right[k][top + SIDE * ROWS : top + SIDE * ROWS + RANK] = proj[1]

    for i in range(PER_CHUNK):
        dx, dz = i // SIDE, i % SIDE
        pieces = []
        for ref, at in ((q_left[dz], dx * PACK), (q_right[dx], dz * PACK)):
            pieces += [ref[at + ROWS : at + PACK, :128], ref[at + ROWS : at + PACK, 128:]]
        bt = jnp.concatenate(pieces, axis=0)
        for side, ref, at in ((0, q_left[dz], dx * PACK), (1, q_right[dx], dz * PACK)):
            value = ref[at : at + ROWS].astype(f32) + keep * mm_t(bt, proj[side])
            m[i * ROWS : (i + 1) * ROWS, side * HALF : (side + 1) * HALF] = value.astype(bf16)

    acc[...] = mm_t(m[:1024], m[:1024])
    acc[...] += mm_t(m[1024:], m[1024:])

    rows = lax.broadcasted_iota(jnp.int32, (FF, FF), 0)
    cols = lax.broadcasted_iota(jnp.int32, (FF, FF), 1)
    whole = acc[...]
    square_sum = jnp.sum(jnp.where(rows == cols, whole, 0.0), axis=(0, 1), keepdims=True)
    inverse = 1.0 / (jnp.sqrt(square_sum) + epsilon)
    gram[...] = ((whole * inverse) * inverse).astype(bf16)

    def factor():
        a = gram[...]
        return (coef_second * a.astype(f32) + coef_third * mm(a, a)).astype(bf16)

    def advance(b):
        a = gram[...]
        half_way = (coef_first * a.astype(f32) + mm(a, b)).astype(bf16)
        gram[...] = (coef_first * half_way.astype(f32) + mm(half_way, b)).astype(bf16)

    b_one[...] = factor()
    advance(b_one[...])
    b = factor()
    q_mat[...] = (
        coef_first * (b_one[...].astype(f32) + b.astype(f32)) + mm(b_one[...], b)
    ).astype(bf16)
    advance(b)
    b = factor()
    q = q_mat[...]
    q_mat[...] = (
        coef_first * q.astype(f32) + coef_first * coef_first * b.astype(f32) + mm(q, b)
    ).astype(bf16)

    for dx in range(SIDE):
        part = m[dx * 512 : (dx + 1) * 512, :]
        value = (inverse * (coef_first**3 * part.astype(f32) + mm(part, q_mat[...]))).astype(bf16)
        for dz in range(SIDE):
            rows = slice(dz * ROWS, (dz + 1) * ROWS)
            b_left[dz][top + dx * ROWS : top + (dx + 1) * ROWS] = value[rows, :HALF]
            b_right[dx][top + dz * ROWS : top + (dz + 1) * ROWS] = value[rows, HALF:]


def orthogonalize(chunk, top, refresh, got):
    return call(
        functools.partial(ortho_kernel, chunk, top),
        [shape(top + BACK, HALF)] * (2 * SIDE),
        [SMEM] + [VMEM] * (2 * SIDE),
        [VMEM] * (2 * SIDE),
        [
            pltpu.VMEM((D, FF), bf16),
            pltpu.VMEM((FF, FF), f32),
            pltpu.VMEM((FF, FF), bf16),
            pltpu.VMEM((FF, FF), bf16),
            pltpu.VMEM((FF, FF), bf16),
        ],
        28,
        8e9,
        5e6,
    )(refresh, *got)


def turn_kernel(top, count, *refs):
    outs = refs[count:]
    for side in range(2):
        got = refs[side * SIDE : (side + 1) * SIDE]
        out = outs[side * SIDE : (side + 1) * SIDE]
        for to in range(SIDE):
            for src in range(SIDE):
                at = top + to * ROWS
                out[to][src * ROWS : (src + 1) * ROWS] = got[src][at : at + ROWS]
                at = SIDE * ROWS + src * RANK
                out[to][at : at + RANK] = got[src][top + SIDE * ROWS : top + BACK]


def turn(top, got, into):
    rows = LAST if into is None else into[0].shape[0]
    into = into or []
    return call(
        functools.partial(turn_kernel, top, len(got) + len(into)),
        [shape(rows, HALF)] * (2 * SIDE),
        [VMEM] * (len(got) + len(into)),
        [VMEM] * (2 * SIDE),
        [],
        16,
        1e3,
        4e6,
        {len(got) + k: k for k in range(len(into))},
    )(*got, *into)


def finish_kernel(chunk, count, chosen, refresh, grads, bank, basis, weights, *refs):
    left, right = refs[:SIDE], refs[SIDE : 2 * SIDE]
    new_bank, new_weights, mom, updated, sems = refs[count:]
    place = position()
    scale_step = step_rate * 0.2 * math.sqrt(max(D, FF))
    pending = []
    for i in range(PER_CHUNK):
        dx, dz = i // SIDE, i % SIDE
        s = chunk * PER_CHUNK + plus(place, dx, dz)
        row = chosen[0, s]
        flag = residual_weight * refresh[s].astype(f32)
        both = halves(basis[s])
        for side, ref, at in ((0, left[dx], dz), (1, right[dz], dx)):
            cols = slice(side * HALF, (side + 1) * HALF)
            ortho = ref[at * ROWS : (at + 1) * ROWS].astype(f32)
            value = weights[s, :, cols].astype(f32) * (1.0 - step_rate * decay_rate) - scale_step * ortho
            updated[i, :, cols] = value.astype(bf16)
            proj = ref[SIDE * ROWS + at * RANK : SIDE * ROWS + (at + 1) * RANK]
            low = mm_t(both, jnp.concatenate([proj, proj], axis=0))
            value = (
                momentum_decay * bank[row, :, cols].astype(f32)
                + low
                + flag * (grads[s, :, cols].astype(f32) - low)
            )
            mom[i, :, cols] = value.astype(bf16)
        for copy in (
            pltpu.make_async_copy(updated.at[i], new_weights.at[s], sems.at[0, i]),
            pltpu.make_async_copy(mom.at[i], new_bank.at[row], sems.at[1, i]),
        ):
            copy.start()
            pending.append(copy)
    for copy in pending:
        copy.wait()


def finish(chunk, chosen, refresh, grads, bank, basis, weights, got, into):
    count = len(got) + len(into)
    return call(
        functools.partial(finish_kernel, chunk, count),
        [shape(CHUNKS * PER_CHUNK, ROWS, FF)] * 2,
        [SMEM] * 2 + [VMEM] * (4 + len(got)) + [HBM] * len(into),
        [HBM] * 2,
        [
            pltpu.VMEM((PER_CHUNK, ROWS, FF), bf16),
            pltpu.VMEM((PER_CHUNK, ROWS, FF), bf16),
            pltpu.SemaphoreType.DMA((2, PER_CHUNK)),
        ],
        30,
        6e8,
        1e7,
        {6 + len(got) + k: k for k in range(len(into))},
    )(chosen, refresh, grads, bank, basis, weights, *got, *into)


def send(array, dx, dz):
    pairs = [
        (x * SIDE + z, ((x + dx) % SIDE) * SIDE + (z + dz) % SIDE)
        for x in range(SIDE)
        for z in range(SIDE)
    ]
    return lax.ppermute(array, "row", pairs)


def exchange(over_x, over_z, sign):
    got_x, got_z = [over_x[0]], [over_z[0]]
    for k in (2, 1, 3):
        got_x.append(send(over_x[k], sign * k, 0))
        got_z.append(send(over_z[k], 0, sign * k))
    order = [0, 2, 1, 3]
    return [got_x[k] for k in order], [got_z[k] for k in order]


def step(sampled, refresh, bank, weights, grads, basis):
    basis_t = jnp.swapaxes(basis, 1, 2)
    state = (sampled, refresh, grads, bank, basis_t)
    kept = tuple(pltpu.with_memory_space_constraint(value, pltpu.HBM) for value in state)

    got = []
    for chunk in range(CHUNKS):
        packed = pack(chunk, 0, *kept)
        got.append(exchange(packed[:SIDE], packed[SIDE:], 1))
    arrived = []
    for chunk in range(CHUNKS):
        got_x, got_z = got[chunk]
        mixed = mix(0, got_x + got_z, None)
        got_x, got_z = exchange(mixed[SIDE:], mixed[:SIDE], 1)
        arrived.append(got_z + got_x)
    backs = [orthogonalize(0, 0, refresh, arrived[0])]
    arrived[1], _ = lax.optimization_barrier((arrived[1], backs[0][0]))
    backs.append(orthogonalize(1, 0, refresh, arrived[1]))
    outs = []
    for chunk in range(CHUNKS):
        back = backs[chunk]
        got_x, got_z = exchange(back[SIDE:], back[:SIDE], -1)
        turned = turn(0, got_z + got_x, None)
        got_x, got_z = exchange(turned[:SIDE], turned[SIDE:], -1)
        outs = list(finish(chunk, *state, weights, got_x + got_z, outs))
    return tuple(outs)


def solution(mesh):
    in_specs = (
        P("expert", None),
        P("expert"),
        P("expert", "row", None),
        P("expert", "row", None),
        P("expert", "row", None),
        P("expert", "row", None),
    )
    out_specs = (P("expert", "row", None), P("expert", "row", None))
    return jax.shard_map(step, mesh=mesh, in_specs=in_specs, out_specs=out_specs, check_vma=False)
```

time: 309 us -> 188 us (0.61)
  the two profiles are of different devices: /device:TPU:64 before, /device:TPU:20 now
where the time goes in v1:
time: 188 us
  starting transfers between devices  124 us (66%)
  waiting for transfers between devices  32.5 us (17%)
  Pallas kernels  30.4 us (16%)
    ppermute x48, starting transfers between devices, send(): return lax.ppermute(array, 'row', pairs)  124 us
    ppermute x48, waiting for transfers between devices, send(): return lax.ppermute(array, 'row', pairs)  32.5 us
    pallas_call x2, Pallas kernels, orthogonalize(): call(functools.partial(ortho_kernel, chunk, top), [shape(top + BACK, HALF...  14.1 us
    pallas_call x2, Pallas kernels, pack(): call(functools.partial(pack_kernel, chunk, top), [shape(top + SIDE * FULL...  7.87 us
    pallas_call x2, Pallas kernels, finish(): call(functools.partial(finish_kernel, chunk, count), [shape(CHUNKS * PER_...  7.57 us
  transfers between devices with their start and end apart: 48, of which 14 were waited for; matrix products, arithmetic and copies ran while one was open for 0% of the time, Pallas kernels for 12%

profile of v1, /device:TPU:20, one launch (start us, length us, event | category | flops | bytes accessed | tf_op | source)
XLA Modules:
  0.0 187.7 jit_solution(14245148255432948865)
XLA Ops:
  0.6 3.9 %shard_map.79 = (bf16[832,256]{1,0:T(8,128)(2,1)S(1)}, bf16[832,256]{1,0:T(8,128)(2,1)S(1)}, bf16[832,256]{1,0:T(8,128)(2,1)S(1)}, bf16[832,256]{1,0:T(8,128)(2,...) custom-call(s32[1,32]{1,0:T(1,128)} %chosen.3, ...), custom_call_target="tpu_custom_call" | custom-call | flops 300000000 | bytes 9000000 | tf_op jit(solution)/shard_map/pallas_call | solution.py:146
  9.7 3.6 %collective-permute-start.16 = (bf16[832,256]{1,0:T(8,128)(2,1)S(1)}, bf16[832,256]{1,0:T(8,128)(2,1)S(1)}, u32[]{:S(2)}, u32[]{:S(2)}) collective-permute-start(bf16[832,256]{1,0:T(8,128)(2,1)S(1)} %get-tuple-element.98), channel_id=1, source_target_pairs={{0,2},{1,3},{2,0},{3,1},{4,6},{5,7},{6,4},{7,5},{8,10},{9,11},{10,... | collective-permute-start | bytes 1277960 | tf_op jit(solution)/shard_map/ppermute | solution.py:364
  13.3 3.9 %shard_map.77 = (bf16[832,256]{1,0:T(8,128)(2,1)S(1)}, bf16[832,256]{1,0:T(8,128)(2,1)S(1)}, bf16[832,256]{1,0:T(8,128)(2,1)S(1)}, bf16[832,256]{1,0:T(8,128)(2,...) custom-call(s32[1,32]{1,0:T(1,128)} %chosen.3, ...), custom_call_target="tpu_custom_call" | custom-call | flops 300000000 | bytes 9000000 | tf_op jit(solution)/shard_map/pallas_call | solution.py:146
  17.4 4.0 %collective-permute-start.17 = (bf16[832,256]{1,0:T(8,128)(2,1)S(1)}, bf16[832,256]{1,0:T(8,128)(2,1)S(1)}, u32[]{:S(2)}, u32[]{:S(2)}) collective-permute-start(bf16[832,256]{1,0:T(8,128)(2,1)S(1)} %get-tuple-element.99), channel_id=1, source_target_pairs={{0,3},{1,0},{2,1},{3,2},{4,7},{5,4},{6,5},{7,6},{8,11},{9,8},{10,9... | collective-permute-start | bytes 1277960 | tf_op jit(solution)/shard_map/ppermute | solution.py:364
  21.4 4.0 %collective-permute-done.13.refs_2_ = bf16[832,256]{1,0:T(8,128)(2,1)S(1)} collective-permute-done((bf16[832,256]{1,0:T(8,128)(2,1)S(1)}, bf16[832,256]{1,0:T(8,128)(2,1)S(1)}, u32[]{:S(2)}, u32[]{:S(2)}) %collective-permute-start.13) | collective-permute-done | bytes 426016 | tf_op jit(solution)/shard_map/ppermute | solution.py:364
  32.6 3.6 %collective-permute-start.4 = (bf16[832,256]{1,0:T(8,128)(2,1)S(1)}, bf16[832,256]{1,0:T(8,128)(2,1)S(1)}, u32[]{:S(2)}, u32[]{:S(2)}) collective-permute-start(bf16[832,256]{1,0:T(8,128)(2,1)S(1)} %get-tuple-element.82), channel_id=1, source_target_pairs={{0,2},{1,3},{2,0},{3,1},{4,6},{5,7},{6,4},{7,5},{8,10},{9,11},{10,... | collective-permute-start | bytes 1277960 | tf_op jit(solution)/shard_map/ppermute | solution.py:364
  36.7 4.1 %collective-permute-start.5 = (bf16[832,256]{1,0:T(8,128)(2,1)S(1)}, bf16[832,256]{1,0:T(8,128)(2,1)S(1)}, u32[]{:S(2)}, u32[]{:S(2)}) collective-permute-start(bf16[832,256]{1,0:T(8,128)(2,1)S(1)} %get-tuple-element.83), channel_id=1, source_target_pairs={{0,3},{1,0},{2,1},{3,2},{4,7},{5,4},{6,5},{7,6},{8,11},{9,8},{10,9... | collective-permute-start | bytes 1277960 | tf_op jit(solution)/shard_map/ppermute | solution.py:364
  41.0 5.1 %collective-permute-done.1.refs_2_ = bf16[832,256]{1,0:T(8,128)(2,1)S(1)} collective-permute-done((bf16[832,256]{1,0:T(8,128)(2,1)S(1)}, bf16[832,256]{1,0:T(8,128)(2,1)S(1)}, u32[]{:S(2)}, u32[]{:S(2)}) %collective-permute-start.1) | collective-permute-done | bytes 426016 | tf_op jit(solution)/shard_map/ppermute | solution.py:364
  48.2 3.9 %collective-permute-start.19 = (bf16[640,256]{1,0:T(8,128)(2,1)S(1)}, bf16[640,256]{1,0:T(8,128)(2,1)S(1)}, u32[]{:S(2)}, u32[]{:S(2)}) collective-permute-start(bf16[640,256]{1,0:T(8,128)(2,1)S(1)} %get-tuple-element.102), channel_id=1, source_target_pairs={{0,2},{1,3},{2,0},{3,1},{4,6},{5,7},{6,4},{7,5},{8,10},{9,11},{10,... | collective-permute-start | bytes 983048 | tf_op jit(solution)/shard_map/ppermute | solution.py:364
  52.8 3.2 %collective-permute-done.4.refs_6_ = bf16[832,256]{1,0:T(8,128)(2,1)S(1)} collective-permute-done((bf16[832,256]{1,0:T(8,128)(2,1)S(1)}, bf16[832,256]{1,0:T(8,128)(2,1)S(1)}, u32[]{:S(2)}, u32[]{:S(2)}) %collective-permute-start.4) | collective-permute-done | bytes 426016 | tf_op jit(solution)/shard_map/ppermute | solution.py:364
  56.0 14.4 %collective-permute-start.22 = (bf16[640,256]{1,0:T(8,128)(2,1)S(1)}, bf16[640,256]{1,0:T(8,128)(2,1)S(1)}, u32[]{:S(2)}, u32[]{:S(2)}) collective-permute-start(bf16[640,256]{1,0:T(8,128)(2,1)S(1)} %get-tuple-element.106), channel_id=1, source_target_pairs={{0,8},{1,9},{2,10},{3,11},{4,12},{5,13},{6,14},{7,15},{8,0},{9,1},... | collective-permute-start | bytes 983048 | tf_op jit(solution)/shard_map/ppermute | solution.py:364
  70.8 5.1 %collective-permute-start.7 = (bf16[640,256]{1,0:T(8,128)(2,1)S(1)}, bf16[640,256]{1,0:T(8,128)(2,1)S(1)}, u32[]{:S(2)}, u32[]{:S(2)}) collective-permute-start(bf16[640,256]{1,0:T(8,128)(2,1)S(1)} %get-tuple-element.86), channel_id=1, source_target_pairs={{0,2},{1,3},{2,0},{3,1},{4,6},{5,7},{6,4},{7,5},{8,10},{9,11},{10,... | collective-permute-start | bytes 983048 | tf_op jit(solution)/shard_map/ppermute | solution.py:364
  80.9 2.6 %collective-permute-start.11 = (bf16[640,256]{1,0:T(8,128)(2,1)S(1)}, bf16[640,256]{1,0:T(8,128)(2,1)S(1)}, u32[]{:S(2)}, u32[]{:S(2)}) collective-permute-start(bf16[640,256]{1,0:T(8,128)(2,1)S(1)} %get-tuple-element.91), channel_id=1, source_target_pairs={{0,12},{1,13},{2,14},{3,15},{4,0},{5,1},{6,2},{7,3},{8,4},{9,5},{1... | collective-permute-start | bytes 983048 | tf_op jit(solution)/shard_map/ppermute | solution.py:364
  83.5 7.1 %shard_map.81 = (bf16[576,256]{1,0:T(8,128)(2,1)S(1)}, bf16[576,256]{1,0:T(8,128)(2,1)S(1)}, bf16[576,256]{1,0:T(8,128)(2,1)S(1)}, bf16[576,256]{1,0:T(8,128)(2,...) custom-call(s32[32]{0:T(128)S(1)} %copy-done.5, ...), custom_call_target="tpu_custom_call" | custom-call | flops 8000000000 | bytes 5000000 | tf_op jit(solution)/shard_map/pallas_call | solution.py:257
  90.6 5.4 %collective-permute-start.36 = (bf16[576,256]{1,0:T(8,128)(2,1)S(1)}, bf16[576,256]{1,0:T(8,128)(2,1)S(1)}, u32[]{:S(2)}, u32[]{:S(2)}) collective-permute-start(bf16[576,256]{1,0:T(8,128)(2,1)S(1)} %get-tuple-element.133), channel_id=1, source_target_pairs={{0,3},{1,0},{2,1},{3,2},{4,7},{5,4},{6,5},{7,6},{8,11},{9,8},{10,9... | collective-permute-start | bytes 884744 | tf_op jit(solution)/shard_map/ppermute | solution.py:364
  99.4 4.6 %collective-permute-done.36.refs_1_ = bf16[576,256]{1,0:T(8,128)(2,1)S(1)} collective-permute-done((bf16[576,256]{1,0:T(8,128)(2,1)S(1)}, bf16[576,256]{1,0:T(8,128)(2,1)S(1)}, u32[]{:S(2)}, u32[]{:S(2)}) %collective-permute-start.36) | collective-permute-done | bytes 294944 | tf_op jit(solution)/shard_map/ppermute | solution.py:364
  104.1 7.1 %shard_map.82 = (bf16[576,256]{1,0:T(8,128)(2,1)S(1)}, bf16[576,256]{1,0:T(8,128)(2,1)S(1)}, bf16[576,256]{1,0:T(8,128)(2,1)S(1)}, bf16[576,256]{1,0:T(8,128)(2,...) custom-call(s32[32]{0:T(128)S(1)} %copy-done.5, ...), custom_call_target="tpu_custom_call" | custom-call | flops 8000000000 | bytes 5000000 | tf_op jit(solution)/shard_map/pallas_call | solution.py:257
  111.2 3.8 %collective-permute-start.24 = (bf16[576,256]{1,0:T(8,128)(2,1)S(1)}, bf16[576,256]{1,0:T(8,128)(2,1)S(1)}, u32[]{:S(2)}, u32[]{:S(2)}) collective-permute-start(bf16[576,256]{1,0:T(8,128)(2,1)S(1)} %get-tuple-element.118), channel_id=1, source_target_pairs={{0,3},{1,0},{2,1},{3,2},{4,7},{5,4},{6,5},{7,6},{8,11},{9,8},{10,9... | collective-permute-start | bytes 884744 | tf_op jit(solution)/shard_map/ppermute | solution.py:364
  116.1 2.9 %collective-permute-start.42 = (bf16[768,256]{1,0:T(8,128)(2,1)S(1)}, bf16[768,256]{1,0:T(8,128)(2,1)S(1)}, u32[]{:S(2)}, u32[]{:S(2)}) collective-permute-start(bf16[768,256]{1,0:T(8,128)(2,1)S(1)} %get-tuple-element.141), channel_id=1, source_target_pairs={{0,12},{1,13},{2,14},{3,15},{4,0},{5,1},{6,2},{7,3},{8,4},{9,5},{1... | collective-permute-start | bytes 1179656 | tf_op jit(solution)/shard_map/ppermute | solution.py:364
  119.1 7.1 %collective-permute-start.43 = (bf16[768,256]{1,0:T(8,128)(2,1)S(1)}, bf16[768,256]{1,0:T(8,128)(2,1)S(1)}, u32[]{:S(2)}, u32[]{:S(2)}) collective-permute-start(bf16[768,256]{1,0:T(8,128)(2,1)S(1)} %get-tuple-element.142), channel_id=1, source_target_pairs={{0,8},{1,9},{2,10},{3,11},{4,12},{5,13},{6,14},{7,15},{8,0},{9,1},... | collective-permute-start | bytes 1179656 | tf_op jit(solution)/shard_map/ppermute | solution.py:364
  126.3 8.2 %collective-permute-start.28 = (bf16[576,256]{1,0:T(8,128)(2,1)S(1)}, bf16[576,256]{1,0:T(8,128)(2,1)S(1)}, u32[]{:S(2)}, u32[]{:S(2)}) collective-permute-start(bf16[576,256]{1,0:T(8,128)(2,1)S(1)} %get-tuple-element.123), channel_id=1, source_target_pairs={{0,8},{1,9},{2,10},{3,11},{4,12},{5,13},{6,14},{7,15},{8,0},{9,1},... | collective-permute-start | bytes 884744 | tf_op jit(solution)/shard_map/ppermute | solution.py:364
  134.5 5.8 %collective-permute-start.29 = (bf16[576,256]{1,0:T(8,128)(2,1)S(1)}, bf16[576,256]{1,0:T(8,128)(2,1)S(1)}, u32[]{:S(2)}, u32[]{:S(2)}) collective-permute-start(bf16[576,256]{1,0:T(8,128)(2,1)S(1)} %get-tuple-element.124), channel_id=1, source_target_pairs={{0,4},{1,5},{2,6},{3,7},{4,8},{5,9},{6,10},{7,11},{8,12},{9,13},{1... | collective-permute-start | bytes 884744 | tf_op jit(solution)/shard_map/ppermute | solution.py:364
  142.5 5.7 %collective-permute-start.44 = (bf16[768,256]{1,0:T(8,128)(2,1)S(1)}, bf16[768,256]{1,0:T(8,128)(2,1)S(1)}, u32[]{:S(2)}, u32[]{:S(2)}) collective-permute-start(bf16[768,256]{1,0:T(8,128)(2,1)S(1)} %get-tuple-element.143), channel_id=1, source_target_pairs={{0,4},{1,5},{2,6},{3,7},{4,8},{5,9},{6,10},{7,11},{8,12},{9,13},{1... | collective-permute-start | bytes 1179656 | tf_op jit(solution)/shard_map/ppermute | solution.py:364
  148.2 5.6 %collective-permute-start.45 = (bf16[768,256]{1,0:T(8,128)(2,1)S(1)}, bf16[768,256]{1,0:T(8,128)(2,1)S(1)}, u32[]{:S(2)}, u32[]{:S(2)}) collective-permute-start(bf16[768,256]{1,0:T(8,128)(2,1)S(1)} %get-tuple-element.145), channel_id=1, source_target_pairs={{0,3},{1,0},{2,1},{3,2},{4,7},{5,4},{6,5},{7,6},{8,11},{9,8},{10,9... | collective-permute-start | bytes 1179656 | tf_op jit(solution)/shard_map/ppermute | solution.py:364
  153.9 2.8 %collective-permute-start.46 = (bf16[768,256]{1,0:T(8,128)(2,1)S(1)}, bf16[768,256]{1,0:T(8,128)(2,1)S(1)}, u32[]{:S(2)}, u32[]{:S(2)}) collective-permute-start(bf16[768,256]{1,0:T(8,128)(2,1)S(1)} %get-tuple-element.146), channel_id=1, source_target_pairs={{0,2},{1,3},{2,0},{3,1},{4,6},{5,7},{6,4},{7,5},{8,10},{9,11},{10,... | collective-permute-start | bytes 1179656 | tf_op jit(solution)/shard_map/ppermute | solution.py:364
  157.1 3.2 %collective-permute-start.31 = (bf16[768,256]{1,0:T(8,128)(2,1)S(1)}, bf16[768,256]{1,0:T(8,128)(2,1)S(1)}, u32[]{:S(2)}, u32[]{:S(2)}) collective-permute-start(bf16[768,256]{1,0:T(8,128)(2,1)S(1)} %get-tuple-element.127), channel_id=1, source_target_pairs={{0,8},{1,9},{2,10},{3,11},{4,12},{5,13},{6,14},{7,15},{8,0},{9,1},... | collective-permute-start | bytes 1179656 | tf_op jit(solution)/shard_map/ppermute | solution.py:364
  160.3 6.2 %collective-permute-start.32 = (bf16[768,256]{1,0:T(8,128)(2,1)S(1)}, bf16[768,256]{1,0:T(8,128)(2,1)S(1)}, u32[]{:S(2)}, u32[]{:S(2)}) collective-permute-start(bf16[768,256]{1,0:T(8,128)(2,1)S(1)} %get-tuple-element.128), channel_id=1, source_target_pairs={{0,4},{1,5},{2,6},{3,7},{4,8},{5,9},{6,10},{7,11},{8,12},{9,13},{1... | collective-permute-start | bytes 1179656 | tf_op jit(solution)/shard_map/ppermute | solution.py:364
  166.6 3.7 %collective-permute-start.33 = (bf16[768,256]{1,0:T(8,128)(2,1)S(1)}, bf16[768,256]{1,0:T(8,128)(2,1)S(1)}, u32[]{:S(2)}, u32[]{:S(2)}) collective-permute-start(bf16[768,256]{1,0:T(8,128)(2,1)S(1)} %get-tuple-element.130), channel_id=1, source_target_pairs={{0,3},{1,0},{2,1},{3,2},{4,7},{5,4},{6,5},{7,6},{8,11},{9,8},{10,9... | collective-permute-start | bytes 1179656 | tf_op jit(solution)/shard_map/ppermute | solution.py:364
  171.3 3.8 %shard_map.85 = (bf16[32,128,512]{2,1,0:T(8,128)(2,1)}, bf16[32,128,512]{2,1,0:T(8,128)(2,1)}) custom-call(s32[1,32]{1,0:T(1,128)S(1)} %copy-done.4, s32[32]{0:T(128)S(1)} %copy-done.5, bf16[32,128,512]{2,1,0:T(8,128)(2,1)S(1)} %copy-done, bf16[32,128,512]{2,1,0:T(8,128)(2,1)S(1)} %copy-done.1, f32[32,64,128]{2,1,0:T(8,128)S(1)} %bitcast.3, ...), custom_call_target="tpu_custom_call" | custom-call | flops 600000000 | bytes 10000000 | tf_op jit(solution)/shard_map/pallas_call | solution.py:341
  175.1 4.7 %collective-permute-done.33.refs_5_ = bf16[768,256]{1,0:T(8,128)(2,1)S(1)} collective-permute-done((bf16[768,256]{1,0:T(8,128)(2,1)S(1)}, bf16[768,256]{1,0:T(8,128)(2,1)S(1)}, u32[]{:S(2)}, u32[]{:S(2)}) %collective-permute-start.33) | collective-permute-done | bytes 393248 | tf_op jit(solution)/shard_map/ppermute | solution.py:364
  179.8 4.0 %collective-permute-done.35.refs_7_ = bf16[768,256]{1,0:T(8,128)(2,1)S(1)} collective-permute-done((bf16[768,256]{1,0:T(8,128)(2,1)S(1)}, bf16[768,256]{1,0:T(8,128)(2,1)S(1)}, u32[]{:S(2)}, u32[]{:S(2)}) %collective-permute-start.35) | collective-permute-done | bytes 393248 | tf_op jit(solution)/shard_map/ppermute | solution.py:364
  183.8 3.8 %shard_map.86 = (bf16[32,128,512]{2,1,0:T(8,128)(2,1)}, bf16[32,128,512]{2,1,0:T(8,128)(2,1)}) custom-call(s32[1,32]{1,0:T(1,128)S(1)} %copy-done.4, s32[32]{0:T(128)S(1)} %copy-done.5, bf16[32,128,512]{2,1,0:T(8,128)(2,1)S(1)} %copy-done, bf16[32,128,512]{2,1,0:T(8,128)(2,1)S(1)} %copy-done.1, ...), custom_call_target="tpu_custom_call", output_to_operand_aliasing={{0}: (14, {}), {1}: (15, {})} | custom-call | flops 600000000 | bytes 10000000 | tf_op jit(solution)/shard_map/pallas_call | solution.py:341
  (86 shorter events, 29.7 us)
Async XLA Ops:
  5.9 19.5 %collective-permute-start.13 = (bf16[832,256]{1,0:T(8,128)(2,1)S(1)}, bf16[832,256]{1,0:T(8,128)(2,1)S(1)}, u32[]{:S(2)}, u32[]{:S(2)}) collective-permute-start(bf16[832,256]{1,0:T(8,128)(2,1)S(1)} %get-tuple-element.94), channel_id=1, source_target_pairs={{0,8},{1,9},{2,10},{3,11},{4,12},{5,13},{6,14},{7,15},{8,0},{9,1},... | collective-permute-start | bytes 1277960 | tf_op jit(solution)/shard_map/ppermute | solution.py:364
  6.7 20.5 %collective-permute-start.14 = (bf16[832,256]{1,0:T(8,128)(2,1)S(1)}, bf16[832,256]{1,0:T(8,128)(2,1)S(1)}, u32[]{:S(2)}, u32[]{:S(2)}) collective-permute-start(bf16[832,256]{1,0:T(8,128)(2,1)S(1)} %get-tuple-element.95), channel_id=1, source_target_pairs={{0,12},{1,13},{2,14},{3,15},{4,0},{5,1},{6,2},{7,3},{8,4},{9,5},{1... | collective-permute-start | bytes 1277960 | tf_op jit(solution)/shard_map/ppermute | solution.py:364
  7.8 20.3 %collective-permute-start.15 = (bf16[832,256]{1,0:T(8,128)(2,1)S(1)}, bf16[832,256]{1,0:T(8,128)(2,1)S(1)}, u32[]{:S(2)}, u32[]{:S(2)}) collective-permute-start(bf16[832,256]{1,0:T(8,128)(2,1)S(1)} %get-tuple-element.97), channel_id=1, source_target_pairs={{0,1},{1,2},{2,3},{3,0},{4,5},{5,6},{6,7},{7,4},{8,9},{9,10},{10,1... | collective-permute-start | bytes 1277960 | tf_op jit(solution)/shard_map/ppermute | solution.py:364
  9.7 21.4 %collective-permute-start.16 = (bf16[832,256]{1,0:T(8,128)(2,1)S(1)}, bf16[832,256]{1,0:T(8,128)(2,1)S(1)}, u32[]{:S(2)}, u32[]{:S(2)}) collective-permute-start(bf16[832,256]{1,0:T(8,128)(2,1)S(1)} %get-tuple-element.98), channel_id=1, source_target_pairs={{0,2},{1,3},{2,0},{3,1},{4,6},{5,7},{6,4},{7,5},{8,10},{9,11},{10,... | collective-permute-start | bytes 1277960 | tf_op jit(solution)/shard_map/ppermute | solution.py:364
  17.4 15.2 %collective-permute-start.17 = (bf16[832,256]{1,0:T(8,128)(2,1)S(1)}, bf16[832,256]{1,0:T(8,128)(2,1)S(1)}, u32[]{:S(2)}, u32[]{:S(2)}) collective-permute-start(bf16[832,256]{1,0:T(8,128)(2,1)S(1)} %get-tuple-element.99), channel_id=1, source_target_pairs={{0,3},{1,0},{2,1},{3,2},{4,7},{5,4},{6,5},{7,6},{8,11},{9,8},{10,9... | collective-permute-start | bytes 1277960 | tf_op jit(solution)/shard_map/ppermute | solution.py:364
  27.2 18.9 %collective-permute-start.1 = (bf16[832,256]{1,0:T(8,128)(2,1)S(1)}, bf16[832,256]{1,0:T(8,128)(2,1)S(1)}, u32[]{:S(2)}, u32[]{:S(2)}) collective-permute-start(bf16[832,256]{1,0:T(8,128)(2,1)S(1)} %get-tuple-element.78), channel_id=1, source_target_pairs={{0,8},{1,9},{2,10},{3,11},{4,12},{5,13},{6,14},{7,15},{8,0},{9,1},... | collective-permute-start | bytes 1277960 | tf_op jit(solution)/shard_map/ppermute | solution.py:364
  28.1 20.1 %collective-permute-start.2 = (bf16[832,256]{1,0:T(8,128)(2,1)S(1)}, bf16[832,256]{1,0:T(8,128)(2,1)S(1)}, u32[]{:S(2)}, u32[]{:S(2)}) collective-permute-start(bf16[832,256]{1,0:T(8,128)(2,1)S(1)} %get-tuple-element.79), channel_id=1, source_target_pairs={{0,12},{1,13},{2,14},{3,15},{4,0},{5,1},{6,2},{7,3},{8,4},{9,5},{1... | collective-permute-start | bytes 1277960 | tf_op jit(solution)/shard_map/ppermute | solution.py:364
  31.1 21.0 %collective-permute-start.3 = (bf16[832,256]{1,0:T(8,128)(2,1)S(1)}, bf16[832,256]{1,0:T(8,128)(2,1)S(1)}, u32[]{:S(2)}, u32[]{:S(2)}) collective-permute-start(bf16[832,256]{1,0:T(8,128)(2,1)S(1)} %get-tuple-element.81), channel_id=1, source_target_pairs={{0,1},{1,2},{2,3},{3,0},{4,5},{5,6},{6,7},{7,4},{8,9},{9,10},{10,1... | collective-permute-start | bytes 1277960 | tf_op jit(solution)/shard_map/ppermute | solution.py:364
  32.6 23.4 %collective-permute-start.4 = (bf16[832,256]{1,0:T(8,128)(2,1)S(1)}, bf16[832,256]{1,0:T(8,128)(2,1)S(1)}, u32[]{:S(2)}, u32[]{:S(2)}) collective-permute-start(bf16[832,256]{1,0:T(8,128)(2,1)S(1)} %get-tuple-element.82), channel_id=1, source_target_pairs={{0,2},{1,3},{2,0},{3,1},{4,6},{5,7},{6,4},{7,5},{8,10},{9,11},{10,... | collective-permute-start | bytes 1277960 | tf_op jit(solution)/shard_map/ppermute | solution.py:364
  36.7 19.3 %collective-permute-start.5 = (bf16[832,256]{1,0:T(8,128)(2,1)S(1)}, bf16[832,256]{1,0:T(8,128)(2,1)S(1)}, u32[]{:S(2)}, u32[]{:S(2)}) collective-permute-start(bf16[832,256]{1,0:T(8,128)(2,1)S(1)} %get-tuple-element.83), channel_id=1, source_target_pairs={{0,3},{1,0},{2,1},{3,2},{4,7},{5,4},{6,5},{7,6},{8,11},{9,8},{10,9... | collective-permute-start | bytes 1277960 | tf_op jit(solution)/shard_map/ppermute | solution.py:364
  46.1 24.4 %collective-permute-start.18 = (bf16[640,256]{1,0:T(8,128)(2,1)S(1)}, bf16[640,256]{1,0:T(8,128)(2,1)S(1)}, u32[]{:S(2)}, u32[]{:S(2)}) collective-permute-start(bf16[640,256]{1,0:T(8,128)(2,1)S(1)} %get-tuple-element.101), channel_id=1, source_target_pairs={{0,1},{1,2},{2,3},{3,0},{4,5},{5,6},{6,7},{7,4},{8,9},{9,10},{10,1... | collective-permute-start | bytes 983048 | tf_op jit(solution)/shard_map/ppermute | solution.py:364
  48.2 22.5 %collective-permute-start.19 = (bf16[640,256]{1,0:T(8,128)(2,1)S(1)}, bf16[640,256]{1,0:T(8,128)(2,1)S(1)}, u32[]{:S(2)}, u32[]{:S(2)}) collective-permute-start(bf16[640,256]{1,0:T(8,128)(2,1)S(1)} %get-tuple-element.102), channel_id=1, source_target_pairs={{0,2},{1,3},{2,0},{3,1},{4,6},{5,7},{6,4},{7,5},{8,10},{9,11},{10,... | collective-permute-start | bytes 983048 | tf_op jit(solution)/shard_map/ppermute | solution.py:364
  52.1 18.7 %collective-permute-start.20 = (bf16[640,256]{1,0:T(8,128)(2,1)S(1)}, bf16[640,256]{1,0:T(8,128)(2,1)S(1)}, u32[]{:S(2)}, u32[]{:S(2)}) collective-permute-start(bf16[640,256]{1,0:T(8,128)(2,1)S(1)} %get-tuple-element.103), channel_id=1, source_target_pairs={{0,3},{1,0},{2,1},{3,2},{4,7},{5,4},{6,5},{7,6},{8,11},{9,8},{10,9... | collective-permute-start | bytes 983048 | tf_op jit(solution)/shard_map/ppermute | solution.py:364
  56.0 19.9 %collective-permute-start.21 = (bf16[640,256]{1,0:T(8,128)(2,1)S(1)}, bf16[640,256]{1,0:T(8,128)(2,1)S(1)}, u32[]{:S(2)}, u32[]{:S(2)}) collective-permute-start(bf16[640,256]{1,0:T(8,128)(2,1)S(1)} %get-tuple-element.105), channel_id=1, source_target_pairs={{0,4},{1,5},{2,6},{3,7},{4,8},{5,9},{6,10},{7,11},{8,12},{9,13},{1... | collective-permute-start | bytes 983048 | tf_op jit(solution)/shard_map/ppermute | solution.py:364
  56.0 20.9 %collective-permute-start.22 = (bf16[640,256]{1,0:T(8,128)(2,1)S(1)}, bf16[640,256]{1,0:T(8,128)(2,1)S(1)}, u32[]{:S(2)}, u32[]{:S(2)}) collective-permute-start(bf16[640,256]{1,0:T(8,128)(2,1)S(1)} %get-tuple-element.106), channel_id=1, source_target_pairs={{0,8},{1,9},{2,10},{3,11},{4,12},{5,13},{6,14},{7,15},{8,0},{9,1},... | collective-permute-start | bytes 983048 | tf_op jit(solution)/shard_map/ppermute | solution.py:364
  70.8 19.8 %collective-permute-start.7 = (bf16[640,256]{1,0:T(8,128)(2,1)S(1)}, bf16[640,256]{1,0:T(8,128)(2,1)S(1)}, u32[]{:S(2)}, u32[]{:S(2)}) collective-permute-start(bf16[640,256]{1,0:T(8,128)(2,1)S(1)} %get-tuple-element.86), channel_id=1, source_target_pairs={{0,2},{1,3},{2,0},{3,1},{4,6},{5,7},{6,4},{7,5},{8,10},{9,11},{10,... | collective-permute-start | bytes 983048 | tf_op jit(solution)/shard_map/ppermute | solution.py:364
  75.9 20.1 %collective-permute-start.8 = (bf16[640,256]{1,0:T(8,128)(2,1)S(1)}, bf16[640,256]{1,0:T(8,128)(2,1)S(1)}, u32[]{:S(2)}, u32[]{:S(2)}) collective-permute-start(bf16[640,256]{1,0:T(8,128)(2,1)S(1)} %get-tuple-element.87), channel_id=1, source_target_pairs={{0,3},{1,0},{2,1},{3,2},{4,7},{5,4},{6,5},{7,6},{8,11},{9,8},{10,9... | collective-permute-start | bytes 983048 | tf_op jit(solution)/shard_map/ppermute | solution.py:364
  76.9 19.2 %collective-permute-start.9 = (bf16[640,256]{1,0:T(8,128)(2,1)S(1)}, bf16[640,256]{1,0:T(8,128)(2,1)S(1)}, u32[]{:S(2)}, u32[]{:S(2)}) collective-permute-start(bf16[640,256]{1,0:T(8,128)(2,1)S(1)} %get-tuple-element.89), channel_id=1, source_target_pairs={{0,4},{1,5},{2,6},{3,7},{4,8},{5,9},{6,10},{7,11},{8,12},{9,13},{1... | collective-permute-start | bytes 983048 | tf_op jit(solution)/shard_map/ppermute | solution.py:364
  78.5 18.5 %collective-permute-start.10 = (bf16[640,256]{1,0:T(8,128)(2,1)S(1)}, bf16[640,256]{1,0:T(8,128)(2,1)S(1)}, u32[]{:S(2)}, u32[]{:S(2)}) collective-permute-start(bf16[640,256]{1,0:T(8,128)(2,1)S(1)} %get-tuple-element.90), channel_id=1, source_target_pairs={{0,8},{1,9},{2,10},{3,11},{4,12},{5,13},{6,14},{7,15},{8,0},{9,1},... | collective-permute-start | bytes 983048 | tf_op jit(solution)/shard_map/ppermute | solution.py:364
  80.9 16.3 %collective-permute-start.11 = (bf16[640,256]{1,0:T(8,128)(2,1)S(1)}, bf16[640,256]{1,0:T(8,128)(2,1)S(1)}, u32[]{:S(2)}, u32[]{:S(2)}) collective-permute-start(bf16[640,256]{1,0:T(8,128)(2,1)S(1)} %get-tuple-element.91), channel_id=1, source_target_pairs={{0,12},{1,13},{2,14},{3,15},{4,0},{5,1},{6,2},{7,3},{8,4},{9,5},{1... | collective-permute-start | bytes 983048 | tf_op jit(solution)/shard_map/ppermute | solution.py:364
  96.0 15.2 %collective-permute-start.37 = (bf16[576,256]{1,0:T(8,128)(2,1)S(1)}, bf16[576,256]{1,0:T(8,128)(2,1)S(1)}, u32[]{:S(2)}, u32[]{:S(2)}) collective-permute-start(bf16[576,256]{1,0:T(8,128)(2,1)S(1)} %get-tuple-element.134), channel_id=1, source_target_pairs={{0,2},{1,3},{2,0},{3,1},{4,6},{5,7},{6,4},{7,5},{8,10},{9,11},{10,... | collective-permute-start | bytes 884744 | tf_op jit(solution)/shard_map/ppermute | solution.py:364
  96.0 18.9 %collective-permute-start.38 = (bf16[576,256]{1,0:T(8,128)(2,1)S(1)}, bf16[576,256]{1,0:T(8,128)(2,1)S(1)}, u32[]{:S(2)}, u32[]{:S(2)}) collective-permute-start(bf16[576,256]{1,0:T(8,128)(2,1)S(1)} %get-tuple-element.135), channel_id=1, source_target_pairs={{0,1},{1,2},{2,3},{3,0},{4,5},{5,6},{6,7},{7,4},{8,9},{9,10},{10,1... | collective-permute-start | bytes 884744 | tf_op jit(solution)/shard_map/ppermute | solution.py:364
  97.0 18.0 %collective-permute-start.39 = (bf16[576,256]{1,0:T(8,128)(2,1)S(1)}, bf16[576,256]{1,0:T(8,128)(2,1)S(1)}, u32[]{:S(2)}, u32[]{:S(2)}) collective-permute-start(bf16[576,256]{1,0:T(8,128)(2,1)S(1)} %get-tuple-element.137), channel_id=1, source_target_pairs={{0,12},{1,13},{2,14},{3,15},{4,0},{5,1},{6,2},{7,3},{8,4},{9,5},{1... | collective-permute-start | bytes 884744 | tf_op jit(solution)/shard_map/ppermute | solution.py:364
  97.1 18.8 %collective-permute-start.40 = (bf16[576,256]{1,0:T(8,128)(2,1)S(1)}, bf16[576,256]{1,0:T(8,128)(2,1)S(1)}, u32[]{:S(2)}, u32[]{:S(2)}) collective-permute-start(bf16[576,256]{1,0:T(8,128)(2,1)S(1)} %get-tuple-element.138), channel_id=1, source_target_pairs={{0,8},{1,9},{2,10},{3,11},{4,12},{5,13},{6,14},{7,15},{8,0},{9,1},... | collective-permute-start | bytes 884744 | tf_op jit(solution)/shard_map/ppermute | solution.py:364
  111.2 15.0 %collective-permute-start.24 = (bf16[576,256]{1,0:T(8,128)(2,1)S(1)}, bf16[576,256]{1,0:T(8,128)(2,1)S(1)}, u32[]{:S(2)}, u32[]{:S(2)}) collective-permute-start(bf16[576,256]{1,0:T(8,128)(2,1)S(1)} %get-tuple-element.118), channel_id=1, source_target_pairs={{0,3},{1,0},{2,1},{3,2},{4,7},{5,4},{6,5},{7,6},{8,11},{9,8},{10,9... | collective-permute-start | bytes 884744 | tf_op jit(solution)/shard_map/ppermute | solution.py:364
  115.0 19.5 %collective-permute-start.26 = (bf16[576,256]{1,0:T(8,128)(2,1)S(1)}, bf16[576,256]{1,0:T(8,128)(2,1)S(1)}, u32[]{:S(2)}, u32[]{:S(2)}) collective-permute-start(bf16[576,256]{1,0:T(8,128)(2,1)S(1)} %get-tuple-element.120), channel_id=1, source_target_pairs={{0,1},{1,2},{2,3},{3,0},{4,5},{5,6},{6,7},{7,4},{8,9},{9,10},{10,1... | collective-permute-start | bytes 884744 | tf_op jit(solution)/shard_map/ppermute | solution.py:364
  116.1 40.7 %collective-permute-start.42 = (bf16[768,256]{1,0:T(8,128)(2,1)S(1)}, bf16[768,256]{1,0:T(8,128)(2,1)S(1)}, u32[]{:S(2)}, u32[]{:S(2)}) collective-permute-start(bf16[768,256]{1,0:T(8,128)(2,1)S(1)} %get-tuple-element.141), channel_id=1, source_target_pairs={{0,12},{1,13},{2,14},{3,15},{4,0},{5,1},{6,2},{7,3},{8,4},{9,5},{1... | collective-permute-start | bytes 1179656 | tf_op jit(solution)/shard_map/ppermute | solution.py:364
  119.1 37.9 %collective-permute-start.43 = (bf16[768,256]{1,0:T(8,128)(2,1)S(1)}, bf16[768,256]{1,0:T(8,128)(2,1)S(1)}, u32[]{:S(2)}, u32[]{:S(2)}) collective-permute-start(bf16[768,256]{1,0:T(8,128)(2,1)S(1)} %get-tuple-element.142), channel_id=1, source_target_pairs={{0,8},{1,9},{2,10},{3,11},{4,12},{5,13},{6,14},{7,15},{8,0},{9,1},... | collective-permute-start | bytes 1179656 | tf_op jit(solution)/shard_map/ppermute | solution.py:364
  126.2 16.3 %collective-permute-start.27 = (bf16[576,256]{1,0:T(8,128)(2,1)S(1)}, bf16[576,256]{1,0:T(8,128)(2,1)S(1)}, u32[]{:S(2)}, u32[]{:S(2)}) collective-permute-start(bf16[576,256]{1,0:T(8,128)(2,1)S(1)} %get-tuple-element.122), channel_id=1, source_target_pairs={{0,12},{1,13},{2,14},{3,15},{4,0},{5,1},{6,2},{7,3},{8,4},{9,5},{1... | collective-permute-start | bytes 884744 | tf_op jit(solution)/shard_map/ppermute | solution.py:364
  126.3 22.0 %collective-permute-start.28 = (bf16[576,256]{1,0:T(8,128)(2,1)S(1)}, bf16[576,256]{1,0:T(8,128)(2,1)S(1)}, u32[]{:S(2)}, u32[]{:S(2)}) collective-permute-start(bf16[576,256]{1,0:T(8,128)(2,1)S(1)} %get-tuple-element.123), channel_id=1, source_target_pairs={{0,8},{1,9},{2,10},{3,11},{4,12},{5,13},{6,14},{7,15},{8,0},{9,1},... | collective-permute-start | bytes 884744 | tf_op jit(solution)/shard_map/ppermute | solution.py:364
  134.5 19.4 %collective-permute-start.29 = (bf16[576,256]{1,0:T(8,128)(2,1)S(1)}, bf16[576,256]{1,0:T(8,128)(2,1)S(1)}, u32[]{:S(2)}, u32[]{:S(2)}) collective-permute-start(bf16[576,256]{1,0:T(8,128)(2,1)S(1)} %get-tuple-element.124), channel_id=1, source_target_pairs={{0,4},{1,5},{2,6},{3,7},{4,8},{5,9},{6,10},{7,11},{8,12},{9,13},{1... | collective-permute-start | bytes 884744 | tf_op jit(solution)/shard_map/ppermute | solution.py:364
  157.1 18.0 %collective-permute-start.31 = (bf16[768,256]{1,0:T(8,128)(2,1)S(1)}, bf16[768,256]{1,0:T(8,128)(2,1)S(1)}, u32[]{:S(2)}, u32[]{:S(2)}) collective-permute-start(bf16[768,256]{1,0:T(8,128)(2,1)S(1)} %get-tuple-element.127), channel_id=1, source_target_pairs={{0,8},{1,9},{2,10},{3,11},{4,12},{5,13},{6,14},{7,15},{8,0},{9,1},... | collective-permute-start | bytes 1179656 | tf_op jit(solution)/shard_map/ppermute | solution.py:364
  (22 other events, 583.8 us)

commit v2 on v1

v2 whole, which is shorter than its diff:
```python
import functools
import math

import jax
import jax.numpy as jnp
from jax import lax
from jax.experimental import pallas as pl
from jax.experimental.pallas import tpu as pltpu
from jax.sharding import PartitionSpec as P


D = 2048
FF = 512
HALF = 256
RANK = 64
ROWS = 128
SIDE = 4
PER_CHUNK = 16
CHUNKS = 2
PACK = ROWS + 16
FULL = PACK + RANK
MIX = SIDE * PACK + RANK
BACK = SIDE * ROWS + RANK
LAST = SIDE * ROWS + SIDE * RANK

momentum_decay = 0.9
residual_weight = 2.0
step_rate = 0.5
decay_rate = 0.1
coef_first = 3.4445
coef_second = -4.775
coef_third = 2.0315
epsilon = 1e-07


SMEM = pl.BlockSpec(memory_space=pltpu.SMEM)
VMEM = pl.BlockSpec(memory_space=pltpu.VMEM)
HBM = pl.BlockSpec(memory_space=pltpu.HBM)
bf16 = jnp.bfloat16
f32 = jnp.float32


def shape(*dims, dtype=bf16):
    return jax.ShapeDtypeStruct(dims, dtype)


def call(kernel, out_shape, in_specs, out_specs, scratch, limit, flops, moved, aliases=None):
    return pl.pallas_call(
        kernel,
        out_shape=out_shape,
        in_specs=in_specs,
        out_specs=out_specs,
        scratch_shapes=scratch,
        input_output_aliases=aliases or {},
        compiler_params=pltpu.CompilerParams(vmem_limit_bytes=limit << 20),
        cost_estimate=pl.CostEstimate(flops=int(flops), bytes_accessed=int(moved), transcendentals=0),
    )


def position():
    me = lax.axis_index("row")
    return lax.div(me, SIDE), lax.rem(me, SIDE)


def plus(place, dx, dz):
    return lax.rem(place[0] + dx, SIDE) * SIDE + lax.rem(place[1] + dz, SIDE)


def mm(a, b):
    return jnp.dot(a, b, preferred_element_type=f32)


def mm_t(a, b):
    return lax.dot_general(a, b, (((0,), (0,)), ((), ())), preferred_element_type=f32)


def halves(value):
    high = value.astype(bf16)
    return jnp.concatenate([high, (value - high.astype(f32)).astype(bf16)], axis=0)


def added(parts):
    total = parts[0].astype(f32)
    for part in parts[1:]:
        total = total + part.astype(f32)
    return total.astype(bf16)


def pack_kernel(chunk, steps, chosen_in, refresh_in, grads, bank, basis, *rest):
    left, right = rest[: len(steps)], rest[len(steps) : 2 * len(steps)]
    g, old, bt, chosen, refresh, sems, flags = rest[2 * len(steps) :]
    place = position()
    base = chunk * PER_CHUNK
    small = (
        pltpu.make_async_copy(chosen_in, chosen, flags.at[0]),
        pltpu.make_async_copy(refresh_in, refresh, flags.at[1]),
    )
    for copy in small:
        copy.start()

    jobs = []
    for n, k in enumerate(steps):
        for j in range(SIDE):
            jobs.append((k * SIDE + j, 0, left[n], j))
            jobs.append((j * SIDE + k, 1, right[n], j))

    def number(i):
        return base + plus(place, i // SIDE, i % SIDE)

    def columns(side):
        return slice(side * HALF, (side + 1) * HALF)

    basis_copies = {}
    block_copies = []
    for i, side, _, _ in jobs:
        if i not in basis_copies:
            basis_copies[i] = pltpu.make_async_copy(basis.at[number(i)], bt.at[i], sems.at[2, 0, i])
            basis_copies[i].start()
        copy = pltpu.make_async_copy(
            grads.at[number(i), :, columns(side)], g.at[i, :, columns(side)], sems.at[0, side, i]
        )
        copy.start()
        block_copies.append([copy])
    for copy in small:
        copy.wait()
    for (i, side, _, _), copies in zip(jobs, block_copies):
        copy = pltpu.make_async_copy(
            bank.at[chosen[0, number(i)], :, columns(side)], old.at[i, :, columns(side)], sems.at[1, side, i]
        )
        copy.start()
        copies.append(copy)

    ready = set()
    for n, (i, side, out, at) in enumerate(jobs):
        if n % 8 == 0:
            for (later, _, _, _), copies in zip(jobs[n : n + 8], block_copies[n : n + 8]):
                for copy in copies:
                    copy.wait()
                if later not in ready:
                    basis_copies[later].wait()
                    ready.add(later)
        flag = residual_weight * refresh[number(i)].astype(f32)
        both = halves(bt[i])
        grad = g[i, :, columns(side)]
        value = momentum_decay * old[i, :, columns(side)].astype(f32) + flag * grad.astype(f32)
        at = at * FULL
        out[at : at + ROWS] = value.astype(bf16)
        first = 32 * side
        out[at + ROWS : at + PACK, :128] = both[first : first + 16]
        out[at + ROWS : at + PACK, 128:] = both[first + 16 : first + 32]
        part = mm(both, grad)
        out[at + PACK : at + FULL] = (part[:RANK] + part[RANK:]).astype(bf16)


def pack(chunk, steps, chosen, refresh, grads, bank, basis):
    outs = call(
        functools.partial(pack_kernel, chunk, steps),
        [shape(SIDE * FULL, HALF)] * (2 * len(steps)),
        [HBM] * 5,
        [VMEM] * (2 * len(steps)),
        [
            pltpu.VMEM((PER_CHUNK, ROWS, FF), bf16),
            pltpu.VMEM((PER_CHUNK, ROWS, FF), bf16),
            pltpu.VMEM((PER_CHUNK, RANK, ROWS), f32),
            pltpu.SMEM((1, CHUNKS * PER_CHUNK), jnp.int32),
            pltpu.SMEM((CHUNKS * PER_CHUNK,), jnp.int32),
            pltpu.SemaphoreType.DMA((3, 2, PER_CHUNK)),
            pltpu.SemaphoreType.DMA((2,)),
        ],
        22,
        1e8 * len(steps),
        3e6 * len(steps),
    )(chosen, refresh, grads, bank, basis)
    return dict(zip(steps, outs[: len(steps)])), dict(zip(steps, outs[len(steps) :]))


def mix_kernel(*refs):
    outs = refs[2 * SIDE :]
    for side in range(2):
        got = refs[side * SIDE : (side + 1) * SIDE]
        out = outs[side * SIDE : (side + 1) * SIDE]
        for to in range(SIDE):
            at = to * FULL
            for src in range(SIDE):
                out[to][src * PACK : (src + 1) * PACK] = got[src][at : at + PACK]
            out[to][SIDE * PACK : MIX] = added([ref[at + PACK : at + FULL] for ref in got])


def mix(got):
    return call(
        mix_kernel,
        [shape(MIX, HALF)] * (2 * SIDE),
        [VMEM] * (2 * SIDE),
        [VMEM] * (2 * SIDE),
        [],
        16,
        1e6,
        6e6,
    )(*got)


def ortho_kernel(chunk, refresh, *refs):
    q_left, q_right = refs[:SIDE], refs[SIDE : 2 * SIDE]
    b_left, b_right = refs[2 * SIDE : 3 * SIDE], refs[3 * SIDE : 4 * SIDE]
    m, acc, gram, f_one, f_two, work = refs[4 * SIDE :]
    place = position()
    keep = 1.0 - residual_weight * refresh[chunk * PER_CHUNK + plus(place, 0, 0)].astype(f32)
    proj = [added([ref[SIDE * PACK : MIX] for ref in q]) for q in (q_left, q_right)]
    near = [(keep * part.astype(f32)).astype(bf16) for part in proj]
    for k in range(SIDE):
        b_left[k][SIDE * ROWS : BACK] = proj[0]
        b_right[k][SIDE * ROWS : BACK] = proj[1]

    for i in range(PER_CHUNK):
        dx, dz = i // SIDE, i % SIDE
        pieces = []
        for ref, at in ((q_left[dz], dx * PACK), (q_right[dx], dz * PACK)):
            pieces += [ref[at + ROWS : at + PACK, :128], ref[at + ROWS : at + PACK, 128:]]
        bt = jnp.concatenate(pieces, axis=0)
        for side, ref, at in ((0, q_left[dz], dx * PACK), (1, q_right[dx], dz * PACK)):
            value = ref[at : at + ROWS].astype(f32) + mm_t(bt, near[side])
            m[i * ROWS : (i + 1) * ROWS, side * HALF : (side + 1) * HALF] = value.astype(bf16)

    acc[...] = mm_t(m[:1024], m[:1024])
    acc[...] += mm_t(m[1024:], m[1024:])

    tile = (ROWS, ROWS)
    diagonal = lax.broadcasted_iota(jnp.int32, tile, 0) == lax.broadcasted_iota(jnp.int32, tile, 1)
    blocks = [slice(k * ROWS, (k + 1) * ROWS) for k in range(FF // ROWS)]
    trace = jnp.zeros(tile, f32)
    for block in blocks:
        trace += jnp.where(diagonal, acc[block, block], 0.0)
    inverse = 1.0 / (jnp.sqrt(jnp.sum(trace, axis=(0, 1), keepdims=True)) + epsilon)
    gram[...] = (acc[...] * (inverse * inverse)).astype(bf16)

    def factor(out):
        for at in range(0, FF, HALF):
            rows = slice(at, at + HALF)
            part = gram[rows, :]
            value = coef_second * part.astype(f32) + coef_third * mm(part, gram[...])
            out[rows, :] = value.astype(bf16)
        for block in blocks:
            part = out[block, block].astype(f32)
            out[block, block] = jnp.where(diagonal, part + coef_first, part).astype(bf16)

    def advance(factor_ref):
        work[...] = mm(gram[...], factor_ref[...]).astype(bf16)
        gram[...] = mm(work[...], factor_ref[...]).astype(bf16)

    factor(f_one)
    advance(f_one)
    factor(f_two)
    advance(f_two)
    work[...] = mm(f_one[...], f_two[...]).astype(bf16)
    factor(f_one)
    f_two[...] = (inverse * mm(work[...], f_one[...])).astype(bf16)

    for dx in range(SIDE):
        value = mm(m[dx * 512 : (dx + 1) * 512, :], f_two[...]).astype(bf16)
        for dz in range(SIDE):
            rows = slice(dz * ROWS, (dz + 1) * ROWS)
            b_left[dz][dx * ROWS : (dx + 1) * ROWS] = value[rows, :HALF]
            b_right[dx][dz * ROWS : (dz + 1) * ROWS] = value[rows, HALF:]


def orthogonalize(chunk, refresh, got):
    return call(
        functools.partial(ortho_kernel, chunk),
        [shape(BACK, HALF)] * (2 * SIDE),
        [SMEM] + [VMEM] * (2 * SIDE),
        [VMEM] * (2 * SIDE),
        [
            pltpu.VMEM((D, FF), bf16),
            pltpu.VMEM((FF, FF), f32),
            pltpu.VMEM((FF, FF), bf16),
            pltpu.VMEM((FF, FF), bf16),
            pltpu.VMEM((FF, FF), bf16),
            pltpu.VMEM((FF, FF), bf16),
        ],
        28,
        8e9,
        5e6,
    )(refresh, *got)


def turn_kernel(*refs):
    outs = refs[2 * SIDE :]
    for side in range(2):
        got = refs[side * SIDE : (side + 1) * SIDE]
        out = outs[side * SIDE : (side + 1) * SIDE]
        for to in range(SIDE):
            for src in range(SIDE):
                out[to][src * ROWS : (src + 1) * ROWS] = got[src][to * ROWS : (to + 1) * ROWS]
                at = SIDE * ROWS + src * RANK
                out[to][at : at + RANK] = got[src][SIDE * ROWS : BACK]


def turn(got):
    return call(
        turn_kernel,
        [shape(LAST, HALF)] * (2 * SIDE),
        [VMEM] * (2 * SIDE),
        [VMEM] * (2 * SIDE),
        [],
        16,
        1e3,
        4e6,
    )(*got)


def finish_kernel(parts, unroll, count, chosen, refresh, grads, bank, basis, weights, *refs):
    new_bank, new_weights, mom, updated, sems = refs[count:]
    place = position()
    scale_step = step_rate * 0.2 * math.sqrt(max(D, FF))

    def blocks(n, j):
        chunk, k = parts[n]
        for side, dx, dz in ((0, k, j), (1, j, k)):
            s = chunk * PER_CHUNK + plus(place, dx, dz)
            yield side, refs[2 * n + side], n * SIDE + j, s, slice(side * HALF, (side + 1) * HALF)

    def copies(side, i, s, cols):
        return (
            pltpu.make_async_copy(updated.at[i, :, cols], new_weights.at[s, :, cols], sems.at[0, side, i]),
            pltpu.make_async_copy(mom.at[i, :, cols], new_bank.at[chosen[0, s], :, cols], sems.at[1, side, i]),
        )

    def fill(n, j):
        for side, ref, i, s, cols in blocks(n, j):
            flag = residual_weight * refresh[s].astype(f32)
            both = halves(basis[s])
            ortho = ref[pl.ds(j * ROWS, ROWS)].astype(f32)
            value = weights[s, :, cols].astype(f32) * (1.0 - step_rate * decay_rate) - scale_step * ortho
            updated[i, :, cols] = value.astype(bf16)
            proj = ref[pl.ds(SIDE * ROWS + j * RANK, RANK)]
            proj = ((1.0 - flag) * proj.astype(f32)).astype(bf16)
            low = mm_t(both, jnp.concatenate([proj, proj], axis=0))
            value = momentum_decay * bank[chosen[0, s], :, cols].astype(f32) + (
                flag * grads[s, :, cols].astype(f32) + low
            )
            mom[i, :, cols] = value.astype(bf16)
            for copy in copies(side, i, s, cols):
                copy.start()

    for n in range(len(parts)):
        if unroll:
            for j in range(SIDE):
                fill(n, j)
        else:

            @pl.loop(0, SIDE // 2)
            def _(j):
                fill(n, 2 * j)
                fill(n, 2 * j + 1)

    for n in range(len(parts)):

        @pl.loop(0, SIDE)
        def _(j):
            for side, _, i, s, cols in blocks(n, j):
                for copy in copies(side, i, s, cols):
                    copy.wait()


def finish(parts, unroll, chosen, refresh, grads, bank, basis, weights, got, into):
    pieces = []
    for chunk, k in parts:
        pieces += [got[chunk][0][k], got[chunk][1][k]]
    count = len(pieces) + len(into)
    return list(
        call(
            functools.partial(finish_kernel, parts, unroll, count),
            [shape(CHUNKS * PER_CHUNK, ROWS, FF)] * 2,
            [SMEM] * 2 + [VMEM] * (4 + len(pieces)) + [HBM] * len(into),
            [HBM] * 2,
            [
                pltpu.VMEM((SIDE * len(parts), ROWS, FF), bf16),
                pltpu.VMEM((SIDE * len(parts), ROWS, FF), bf16),
                pltpu.SemaphoreType.DMA((2, 2, SIDE * len(parts))),
            ],
            30,
            1.5e8 * len(parts),
            2.5e6 * len(parts),
            {6 + len(pieces) + k: k for k in range(len(into))},
        )(chosen, refresh, grads, bank, basis, weights, *pieces, *into)
    )


def send(array, dx, dz):
    pairs = [
        (x * SIDE + z, ((x + dx) % SIDE) * SIDE + (z + dz) % SIDE)
        for x in range(SIDE)
        for z in range(SIDE)
    ]
    return lax.ppermute(array, "row", pairs)


STARTS = (("x", 2), ("z", 2), ("x", 1), ("z", 1), ("x", 3), ("z", 3))


def exchange(over_x, over_z, sign):
    got_x, got_z = [over_x[0], None, None, None], [over_z[0], None, None, None]
    for axis, k in STARTS:
        if axis == "x":
            got_x[k] = send(over_x[k], sign * k, 0)
        else:
            got_z[k] = send(over_z[k], 0, sign * k)
    return got_x, got_z


def step(sampled, refresh, bank, weights, grads, basis):
    basis_t = jnp.swapaxes(basis, 1, 2)
    state = (sampled, refresh, grads, bank, basis_t)
    kept = tuple(pltpu.with_memory_space_constraint(value, pltpu.HBM) for value in state)

    got = []
    left, right = pack(0, (2,), *kept)
    more_left, more_right = pack(0, (1, 3, 0), *state)
    got.append(exchange({**left, **more_left}, {**right, **more_right}, 1))
    left, right = pack(1, (2, 1, 3, 0), *state)
    got.append(exchange(left, right, 1))
    arrived = []
    for chunk in range(2):
        got_x, got_z = got[chunk]
        mixed = mix(got_x + got_z)
        got_x, got_z = exchange(mixed[SIDE:], mixed[:SIDE], 1)
        arrived.append(got_z + got_x)
    backs = [orthogonalize(0, refresh, arrived[0])]
    arrived[1], _ = lax.optimization_barrier((arrived[1], backs[0][0]))
    backs.append(orthogonalize(1, refresh, arrived[1]))
    last = []
    for chunk in range(2):
        back = backs[chunk]
        got_x, got_z = exchange(back[SIDE:], back[:SIDE], -1)
        turned = turn(got_z + got_x)
        last.append(exchange(turned[:SIDE], turned[SIDE:], -1))
    outs = finish(((0, 0), (0, 2)), False, *state, weights, last, [])
    outs = finish(((0, 1), (0, 3), (1, 0), (1, 2)), True, *state, weights, last, outs)
    outs = finish(((1, 1), (1, 3)), True, *state, weights, last, outs)
    return tuple(outs)


def solution(mesh):
    in_specs = (
        P("expert", None),
        P("expert"),
        P("expert", "row", None),
        P("expert", "row", None),
        P("expert", "row", None),
        P("expert", "row", None),
    )
    out_specs = (P("expert", "row", None), P("expert", "row", None))
    return jax.shard_map(step, mesh=mesh, in_specs=in_specs, out_specs=out_specs, check_vma=False)
```

time: 188 us -> 176 us (0.936)
  the two profiles are of different devices: /device:TPU:20 before, /device:TPU:64 now
where the time goes in v2:
time: 176 us; the launch traced here: 173 us
  starting transfers between devices  102 us (58%)
  waiting for transfers between devices  35.6 us (20%)
  Pallas kernels  34.8 us (20%)
    ppermute x48, starting transfers between devices, send(): return lax.ppermute(array, 'row', pairs)  102 us
    ppermute x48, waiting for transfers between devices, send(): return lax.ppermute(array, 'row', pairs)  35.6 us
    pallas_call x2, Pallas kernels, orthogonalize(): call(functools.partial(ortho_kernel, chunk), [shape(BACK, HALF)] * (2 * S...  13.5 us
    pallas_call x3, Pallas kernels, pack(): call(functools.partial(pack_kernel, chunk, steps), [shape(SIDE * FULL, HA...  10.8 us
    pallas_call x3, Pallas kernels, finish(): call(functools.partial(finish_kernel, parts, unroll, count), [shape(CHUNK...  9.64 us
  transfers between devices with their start and end apart: 48, of which 12 were waited for; matrix products, arithmetic and copies ran while one was open for 0% of the time, Pallas kernels for 16%

profile of v2, /device:TPU:64, one launch (start us, length us, event | category | flops | bytes accessed | tf_op | source)
XLA Modules:
  0.0 173.5 jit_solution(15038078391931882333)
XLA Ops:
  0.7 3.7 %shard_map.80 = (bf16[832,256]{1,0:T(8,128)(2,1)S(1)}, bf16[832,256]{1,0:T(8,128)(2,1)S(1)}) custom-call(s32[1,32]{1,0:T(1,128)} %chosen.5, s32[32]{0:T(128)} %refresh.9, bf16[32,128,512]{2,1,0:T(8,128)(2,1)} %grads.11, bf16[32,128,512]{2,1,0:T(8,128)(2,1)} %bank.11, f32[32,64,128]{2,1,0:T(8,128)} %bitcast.1), custom_call_target="tpu_custom_call" | custom-call | flops 100000000 | bytes 3000000 | tf_op jit(solution)/shard_map/pallas_call | solution.py:156
  4.4 3.1 %collective-permute-start.13 = (bf16[832,256]{1,0:T(8,128)(2,1)S(1)}, bf16[832,256]{1,0:T(8,128)(2,1)S(1)}, u32[]{:S(2)}, u32[]{:S(2)}) collective-permute-start(bf16[832,256]{1,0:T(8,128)(2,1)S(1)} %get-tuple-element.96), channel_id=1, source_target_pairs={{0,8},{1,9},{2,10},{3,11},{4,12},{5,13},{6,14},{7,15},{8,0},{9,1},... | collective-permute-start | bytes 1277960 | tf_op jit(solution)/shard_map/ppermute | solution.py:395
  7.5 3.3 %shard_map.79 = (bf16[832,256]{1,0:T(8,128)(2,1)S(1)}, bf16[832,256]{1,0:T(8,128)(2,1)S(1)}, bf16[832,256]{1,0:T(8,128)(2,1)S(1)}, bf16[832,256]{1,0:T(8,128)(2,...) custom-call(s32[1,32]{1,0:T(1,128)S(1)} %copy-done.4, s32[32]{0:T(128)S(1)} %copy-done.5, ...), custom_call_target="tpu_custom_call" | custom-call | flops 300000000 | bytes 9000000 | tf_op jit(solution)/shard_map/pallas_call | solution.py:156
  11.5 2.6 %collective-permute-start.14 = (bf16[832,256]{1,0:T(8,128)(2,1)S(1)}, bf16[832,256]{1,0:T(8,128)(2,1)S(1)}, u32[]{:S(2)}, u32[]{:S(2)}) collective-permute-start(bf16[832,256]{1,0:T(8,128)(2,1)S(1)} %get-tuple-element.97), channel_id=1, source_target_pairs={{0,12},{1,13},{2,14},{3,15},{4,0},{5,1},{6,2},{7,3},{8,4},{9,5},{1... | collective-permute-start | bytes 1277960 | tf_op jit(solution)/shard_map/ppermute | solution.py:395
  14.1 2.2 %collective-permute-start.15 = (bf16[832,256]{1,0:T(8,128)(2,1)S(1)}, bf16[832,256]{1,0:T(8,128)(2,1)S(1)}, u32[]{:S(2)}, u32[]{:S(2)}) collective-permute-start(bf16[832,256]{1,0:T(8,128)(2,1)S(1)} %get-tuple-element.99), channel_id=1, source_target_pairs={{0,1},{1,2},{2,3},{3,0},{4,5},{5,6},{6,7},{7,4},{8,9},{9,10},{10,1... | collective-permute-start | bytes 1277960 | tf_op jit(solution)/shard_map/ppermute | solution.py:395
  16.3 3.9 %shard_map.77 = (bf16[832,256]{1,0:T(8,128)(2,1)S(1)}, bf16[832,256]{1,0:T(8,128)(2,1)S(1)}, bf16[832,256]{1,0:T(8,128)(2,1)S(1)}, bf16[832,256]{1,0:T(8,128)(2,...) custom-call(s32[1,32]{1,0:T(1,128)S(1)} %copy-done.4, ...), custom_call_target="tpu_custom_call" | custom-call | flops 400000000 | bytes 12000000 | tf_op jit(solution)/shard_map/pallas_call | solution.py:156
  22.3 4.5 %collective-permute-done.12.refs_1_ = bf16[832,256]{1,0:T(8,128)(2,1)S(1)} collective-permute-done((bf16[832,256]{1,0:T(8,128)(2,1)S(1)}, bf16[832,256]{1,0:T(8,128)(2,1)S(1)}, u32[]{:S(2)}, u32[]{:S(2)}) %collective-permute-start.12) | collective-permute-done | bytes 426016 | tf_op jit(solution)/shard_map/ppermute | solution.py:395
  26.9 2.9 %collective-permute-start.1 = (bf16[832,256]{1,0:T(8,128)(2,1)S(1)}, bf16[832,256]{1,0:T(8,128)(2,1)S(1)}, u32[]{:S(2)}, u32[]{:S(2)}) collective-permute-start(bf16[832,256]{1,0:T(8,128)(2,1)S(1)} %get-tuple-element.80), channel_id=1, source_target_pairs={{0,8},{1,9},{2,10},{3,11},{4,12},{5,13},{6,14},{7,15},{8,0},{9,1},... | collective-permute-start | bytes 1277960 | tf_op jit(solution)/shard_map/ppermute | solution.py:395
  29.8 2.2 %collective-permute-start.2 = (bf16[832,256]{1,0:T(8,128)(2,1)S(1)}, bf16[832,256]{1,0:T(8,128)(2,1)S(1)}, u32[]{:S(2)}, u32[]{:S(2)}) collective-permute-start(bf16[832,256]{1,0:T(8,128)(2,1)S(1)} %get-tuple-element.81), channel_id=1, source_target_pairs={{0,12},{1,13},{2,14},{3,15},{4,0},{5,1},{6,2},{7,3},{8,4},{9,5},{1... | collective-permute-start | bytes 1277960 | tf_op jit(solution)/shard_map/ppermute | solution.py:395
  33.7 3.2 %collective-permute-done.refs_1_ = bf16[832,256]{1,0:T(8,128)(2,1)S(1)} collective-permute-done((bf16[832,256]{1,0:T(8,128)(2,1)S(1)}, bf16[832,256]{1,0:T(8,128)(2,1)S(1)}, u32[]{:S(2)}, u32[]{:S(2)}) %collective-permute-start) | collective-permute-done | bytes 426016 | tf_op jit(solution)/shard_map/ppermute | solution.py:395
  36.9 8.4 %collective-permute-start.5 = (bf16[832,256]{1,0:T(8,128)(2,1)S(1)}, bf16[832,256]{1,0:T(8,128)(2,1)S(1)}, u32[]{:S(2)}, u32[]{:S(2)}) collective-permute-start(bf16[832,256]{1,0:T(8,128)(2,1)S(1)} %get-tuple-element.85), channel_id=1, source_target_pairs={{0,3},{1,0},{2,1},{3,2},{4,7},{5,4},{6,5},{7,6},{8,11},{9,8},{10,9... | collective-permute-start | bytes 1277960 | tf_op jit(solution)/shard_map/ppermute | solution.py:395
  49.4 4.0 %collective-permute-done.4.refs_6_ = bf16[832,256]{1,0:T(8,128)(2,1)S(1)} collective-permute-done((bf16[832,256]{1,0:T(8,128)(2,1)S(1)}, bf16[832,256]{1,0:T(8,128)(2,1)S(1)}, u32[]{:S(2)}, u32[]{:S(2)}) %collective-permute-start.4) | collective-permute-done | bytes 426016 | tf_op jit(solution)/shard_map/ppermute | solution.py:395
  53.6 6.9 %collective-permute-done.5.refs_7_ = bf16[832,256]{1,0:T(8,128)(2,1)S(1)} collective-permute-done((bf16[832,256]{1,0:T(8,128)(2,1)S(1)}, bf16[832,256]{1,0:T(8,128)(2,1)S(1)}, u32[]{:S(2)}, u32[]{:S(2)}) %collective-permute-start.5) | collective-permute-done | bytes 426016 | tf_op jit(solution)/shard_map/ppermute | solution.py:395
  60.8 4.0 %collective-permute-done.18.refs_1_ = bf16[640,256]{1,0:T(8,128)(2,1)S(1)} collective-permute-done((bf16[640,256]{1,0:T(8,128)(2,1)S(1)}, bf16[640,256]{1,0:T(8,128)(2,1)S(1)}, u32[]{:S(2)}, u32[]{:S(2)}) %collective-permute-start.18) | collective-permute-done | bytes 327712 | tf_op jit(solution)/shard_map/ppermute | solution.py:395
  66.3 3.7 %collective-permute-start.7 = (bf16[640,256]{1,0:T(8,128)(2,1)S(1)}, bf16[640,256]{1,0:T(8,128)(2,1)S(1)}, u32[]{:S(2)}, u32[]{:S(2)}) collective-permute-start(bf16[640,256]{1,0:T(8,128)(2,1)S(1)} %get-tuple-element.88), channel_id=1, source_target_pairs={{0,2},{1,3},{2,0},{3,1},{4,6},{5,7},{6,4},{7,5},{8,10},{9,11},{10,... | collective-permute-start | bytes 983048 | tf_op jit(solution)/shard_map/ppermute | solution.py:395
  70.1 2.6 %collective-permute-start.8 = (bf16[640,256]{1,0:T(8,128)(2,1)S(1)}, bf16[640,256]{1,0:T(8,128)(2,1)S(1)}, u32[]{:S(2)}, u32[]{:S(2)}) collective-permute-start(bf16[640,256]{1,0:T(8,128)(2,1)S(1)} %get-tuple-element.89), channel_id=1, source_target_pairs={{0,3},{1,0},{2,1},{3,2},{4,7},{5,4},{6,5},{7,6},{8,11},{9,8},{10,9... | collective-permute-start | bytes 983048 | tf_op jit(solution)/shard_map/ppermute | solution.py:395
  77.2 6.7 %shard_map.82 = (bf16[576,256]{1,0:T(8,128)(2,1)S(1)}, bf16[576,256]{1,0:T(8,128)(2,1)S(1)}, bf16[576,256]{1,0:T(8,128)(2,1)S(1)}, bf16[576,256]{1,0:T(8,128)(2,...) custom-call(s32[32]{0:T(128)S(1)} %copy-done.5, ...), custom_call_target="tpu_custom_call" | custom-call | flops 8000000000 | bytes 5000000 | tf_op jit(solution)/shard_map/pallas_call | solution.py:267
  84.8 6.2 %collective-permute-start.35 = (bf16[576,256]{1,0:T(8,128)(2,1)S(1)}, bf16[576,256]{1,0:T(8,128)(2,1)S(1)}, u32[]{:S(2)}, u32[]{:S(2)}) collective-permute-start(bf16[576,256]{1,0:T(8,128)(2,1)S(1)} %get-tuple-element.132), channel_id=1, source_target_pairs={{0,2},{1,3},{2,0},{3,1},{4,6},{5,7},{6,4},{7,5},{8,10},{9,11},{10,... | collective-permute-start | bytes 884744 | tf_op jit(solution)/shard_map/ppermute | solution.py:395
  91.0 2.5 %collective-permute-start.36 = (bf16[576,256]{1,0:T(8,128)(2,1)S(1)}, bf16[576,256]{1,0:T(8,128)(2,1)S(1)}, u32[]{:S(2)}, u32[]{:S(2)}) collective-permute-start(bf16[576,256]{1,0:T(8,128)(2,1)S(1)} %get-tuple-element.133), channel_id=1, source_target_pairs={{0,1},{1,2},{2,3},{3,0},{4,5},{5,6},{6,7},{7,4},{8,9},{9,10},{10,1... | collective-permute-start | bytes 884744 | tf_op jit(solution)/shard_map/ppermute | solution.py:395
  94.7 2.5 %collective-permute-start.38 = (bf16[576,256]{1,0:T(8,128)(2,1)S(1)}, bf16[576,256]{1,0:T(8,128)(2,1)S(1)}, u32[]{:S(2)}, u32[]{:S(2)}) collective-permute-start(bf16[576,256]{1,0:T(8,128)(2,1)S(1)} %get-tuple-element.136), channel_id=1, source_target_pairs={{0,8},{1,9},{2,10},{3,11},{4,12},{5,13},{6,14},{7,15},{8,0},{9,1},... | collective-permute-start | bytes 884744 | tf_op jit(solution)/shard_map/ppermute | solution.py:395
  98.6 6.7 %shard_map.83 = (bf16[576,256]{1,0:T(8,128)(2,1)S(1)}, bf16[576,256]{1,0:T(8,128)(2,1)S(1)}, bf16[576,256]{1,0:T(8,128)(2,1)S(1)}, bf16[576,256]{1,0:T(8,128)(2,...) custom-call(s32[32]{0:T(128)S(1)} %copy-done.5, ...), custom_call_target="tpu_custom_call" | custom-call | flops 8000000000 | bytes 5000000 | tf_op jit(solution)/shard_map/pallas_call | solution.py:267
  109.4 2.3 %collective-permute-start.40 = (bf16[768,256]{1,0:T(8,128)(2,1)S(1)}, bf16[768,256]{1,0:T(8,128)(2,1)S(1)}, u32[]{:S(2)}, u32[]{:S(2)}) collective-permute-start(bf16[768,256]{1,0:T(8,128)(2,1)S(1)} %get-tuple-element.138), channel_id=1, source_target_pairs={{0,12},{1,13},{2,14},{3,15},{4,0},{5,1},{6,2},{7,3},{8,4},{9,5},{1... | collective-permute-start | bytes 1179656 | tf_op jit(solution)/shard_map/ppermute | solution.py:395
  112.8 4.4 %collective-permute-start.27 = (bf16[576,256]{1,0:T(8,128)(2,1)S(1)}, bf16[576,256]{1,0:T(8,128)(2,1)S(1)}, u32[]{:S(2)}, u32[]{:S(2)}) collective-permute-start(bf16[576,256]{1,0:T(8,128)(2,1)S(1)} %get-tuple-element.124), channel_id=1, source_target_pairs={{0,12},{1,13},{2,14},{3,15},{4,0},{5,1},{6,2},{7,3},{8,4},{9,5},{1... | collective-permute-start | bytes 884744 | tf_op jit(solution)/shard_map/ppermute | solution.py:395
  120.1 8.7 %collective-permute-done.27.refs_5_ = bf16[576,256]{1,0:T(8,128)(2,1)S(1)} collective-permute-done((bf16[576,256]{1,0:T(8,128)(2,1)S(1)}, bf16[576,256]{1,0:T(8,128)(2,1)S(1)}, u32[]{:S(2)}, u32[]{:S(2)}) %collective-permute-start.27) | collective-permute-done | bytes 294944 | tf_op jit(solution)/shard_map/ppermute | solution.py:395
  128.8 9.9 %collective-permute-start.43 = (bf16[768,256]{1,0:T(8,128)(2,1)S(1)}, bf16[768,256]{1,0:T(8,128)(2,1)S(1)}, u32[]{:S(2)}, u32[]{:S(2)}) collective-permute-start(bf16[768,256]{1,0:T(8,128)(2,1)S(1)} %get-tuple-element.141), channel_id=1, source_target_pairs={{0,1},{1,2},{2,3},{3,0},{4,5},{5,6},{6,7},{7,4},{8,9},{9,10},{10,1... | collective-permute-start | bytes 1179656 | tf_op jit(solution)/shard_map/ppermute | solution.py:395
  139.0 3.6 %collective-permute-start.44 = (bf16[768,256]{1,0:T(8,128)(2,1)S(1)}, bf16[768,256]{1,0:T(8,128)(2,1)S(1)}, u32[]{:S(2)}, u32[]{:S(2)}) collective-permute-start(bf16[768,256]{1,0:T(8,128)(2,1)S(1)} %get-tuple-element.144), channel_id=1, source_target_pairs={{0,8},{1,9},{2,10},{3,11},{4,12},{5,13},{6,14},{7,15},{8,0},{9,1},... | collective-permute-start | bytes 1179656 | tf_op jit(solution)/shard_map/ppermute | solution.py:395
  142.6 3.5 %collective-permute-start.45 = (bf16[768,256]{1,0:T(8,128)(2,1)S(1)}, bf16[768,256]{1,0:T(8,128)(2,1)S(1)}, u32[]{:S(2)}, u32[]{:S(2)}) collective-permute-start(bf16[768,256]{1,0:T(8,128)(2,1)S(1)} %get-tuple-element.145), channel_id=1, source_target_pairs={{0,2},{1,3},{2,0},{3,1},{4,6},{5,7},{6,4},{7,5},{8,10},{9,11},{10,... | collective-permute-start | bytes 1179656 | tf_op jit(solution)/shard_map/ppermute | solution.py:395
  146.8 14.4 %collective-permute-start.30 = (bf16[768,256]{1,0:T(8,128)(2,1)S(1)}, bf16[768,256]{1,0:T(8,128)(2,1)S(1)}, u32[]{:S(2)}, u32[]{:S(2)}) collective-permute-start(bf16[768,256]{1,0:T(8,128)(2,1)S(1)} %get-tuple-element.127), channel_id=1, source_target_pairs={{0,12},{1,13},{2,14},{3,15},{4,0},{5,1},{6,2},{7,3},{8,4},{9,5},{1... | collective-permute-start | bytes 1179656 | tf_op jit(solution)/shard_map/ppermute | solution.py:395
  161.3 2.3 %collective-permute-start.33 = (bf16[768,256]{1,0:T(8,128)(2,1)S(1)}, bf16[768,256]{1,0:T(8,128)(2,1)S(1)}, u32[]{:S(2)}, u32[]{:S(2)}) collective-permute-start(bf16[768,256]{1,0:T(8,128)(2,1)S(1)} %get-tuple-element.130), channel_id=1, source_target_pairs={{0,1},{1,2},{2,3},{3,0},{4,5},{5,6},{6,7},{7,4},{8,9},{9,10},{10,1... | collective-permute-start | bytes 1179656 | tf_op jit(solution)/shard_map/ppermute | solution.py:395
  163.6 2.9 %shard_map.86 = (bf16[32,128,512]{2,1,0:T(8,128)(2,1)}, bf16[32,128,512]{2,1,0:T(8,128)(2,1)}) custom-call(s32[1,32]{1,0:T(1,128)S(1)} %copy-done.4, s32[32]{0:T(128)S(1)} %copy-done.5, bf16[32,128,512]{2,1,0:T(8,128)(2,1)S(1)} %copy-done, bf16[32,128,512]{2,1,0:T(8,128)(2,1)S(1)} %copy-done.1, f32[32,64,128]{2,1,0:T(8,128)S(1)} %bitcast.4, ...), custom_call_target="tpu_custom_call" | custom-call | flops 300000000 | bytes 5000000 | tf_op jit(solution)/shard_map/pallas_call | solution.py:371
  166.5 4.1 %shard_map.87 = (bf16[32,128,512]{2,1,0:T(8,128)(2,1)}, bf16[32,128,512]{2,1,0:T(8,128)(2,1)}) custom-call(s32[1,32]{1,0:T(1,128)S(1)} %copy-done.4, s32[32]{0:T(128)S(1)} %copy-done.5, bf16[32,128,512]{2,1,0:T(8,128)(2,1)S(1)} %copy-done, bf16[32,128,512]{2,1,0:T(8,128)(2,1)S(1)} %copy-done.1, ...), custom_call_target="tpu_custom_call", output_to_operand_aliasing={{0}: (14, {}), {1}: (15, {})} | custom-call | flops 600000000 | bytes 10000000 | tf_op jit(solution)/shard_map/pallas_call | solution.py:371
  170.6 2.6 %shard_map.88 = (bf16[32,128,512]{2,1,0:T(8,128)(2,1)}, bf16[32,128,512]{2,1,0:T(8,128)(2,1)}) custom-call(s32[1,32]{1,0:T(1,128)S(1)} %copy-done.4, s32[32]{0:T(128)S(1)} %copy-done.5, bf16[32,128,512]{2,1,0:T(8,128)(2,1)S(1)} %copy-done, bf16[32,128,512]{2,1,0:T(8,128)(2,1)S(1)} %copy-done.1, ...), custom_call_target="tpu_custom_call", output_to_operand_aliasing={{0}: (10, {}), {1}: (11, {})} | custom-call | flops 300000000 | bytes 5000000 | tf_op jit(solution)/shard_map/pallas_call | solution.py:371
  (88 shorter events, 27.5 us)
Async XLA Ops:
  4.4 15.7 %collective-permute-start.13 = (bf16[832,256]{1,0:T(8,128)(2,1)S(1)}, bf16[832,256]{1,0:T(8,128)(2,1)S(1)}, u32[]{:S(2)}, u32[]{:S(2)}) collective-permute-start(bf16[832,256]{1,0:T(8,128)(2,1)S(1)} %get-tuple-element.96), channel_id=1, source_target_pairs={{0,8},{1,9},{2,10},{3,11},{4,12},{5,13},{6,14},{7,15},{8,0},{9,1},... | collective-permute-start | bytes 1277960 | tf_op jit(solution)/shard_map/ppermute | solution.py:395
  7.5 14.2 %collective-permute-start.16 = (bf16[832,256]{1,0:T(8,128)(2,1)S(1)}, bf16[832,256]{1,0:T(8,128)(2,1)S(1)}, u32[]{:S(2)}, u32[]{:S(2)}) collective-permute-start(bf16[832,256]{1,0:T(8,128)(2,1)S(1)} %get-tuple-element.100), channel_id=1, source_target_pairs={{0,2},{1,3},{2,0},{3,1},{4,6},{5,7},{6,4},{7,5},{8,10},{9,11},{10,... | collective-permute-start | bytes 1277960 | tf_op jit(solution)/shard_map/ppermute | solution.py:395
  10.8 16.1 %collective-permute-start.12 = (bf16[832,256]{1,0:T(8,128)(2,1)S(1)}, bf16[832,256]{1,0:T(8,128)(2,1)S(1)}, u32[]{:S(2)}, u32[]{:S(2)}) collective-permute-start(bf16[832,256]{1,0:T(8,128)(2,1)S(1)} %get-tuple-element.95), channel_id=1, source_target_pairs={{0,4},{1,5},{2,6},{3,7},{4,8},{5,9},{6,10},{7,11},{8,12},{9,13},{1... | collective-permute-start | bytes 1277960 | tf_op jit(solution)/shard_map/ppermute | solution.py:395
  11.5 18.3 %collective-permute-start.14 = (bf16[832,256]{1,0:T(8,128)(2,1)S(1)}, bf16[832,256]{1,0:T(8,128)(2,1)S(1)}, u32[]{:S(2)}, u32[]{:S(2)}) collective-permute-start(bf16[832,256]{1,0:T(8,128)(2,1)S(1)} %get-tuple-element.97), channel_id=1, source_target_pairs={{0,12},{1,13},{2,14},{3,15},{4,0},{5,1},{6,2},{7,3},{8,4},{9,5},{1... | collective-permute-start | bytes 1277960 | tf_op jit(solution)/shard_map/ppermute | solution.py:395
  14.1 17.9 %collective-permute-start.15 = (bf16[832,256]{1,0:T(8,128)(2,1)S(1)}, bf16[832,256]{1,0:T(8,128)(2,1)S(1)}, u32[]{:S(2)}, u32[]{:S(2)}) collective-permute-start(bf16[832,256]{1,0:T(8,128)(2,1)S(1)} %get-tuple-element.99), channel_id=1, source_target_pairs={{0,1},{1,2},{2,3},{3,0},{4,5},{5,6},{6,7},{7,4},{8,9},{9,10},{10,1... | collective-permute-start | bytes 1277960 | tf_op jit(solution)/shard_map/ppermute | solution.py:395
  21.7 15.1 %collective-permute-start = (bf16[832,256]{1,0:T(8,128)(2,1)S(1)}, bf16[832,256]{1,0:T(8,128)(2,1)S(1)}, u32[]{:S(2)}, u32[]{:S(2)}) collective-permute-start(bf16[832,256]{1,0:T(8,128)(2,1)S(1)} %get-tuple-element.79), channel_id=1, source_target_pairs={{0,4},{1,5},{2,6},{3,7},{4,8},{5,9},{6,10},{7,11},{8,12},{9,13},{1... | collective-permute-start | bytes 1277960 | tf_op jit(solution)/shard_map/ppermute | solution.py:395
  26.9 18.6 %collective-permute-start.1 = (bf16[832,256]{1,0:T(8,128)(2,1)S(1)}, bf16[832,256]{1,0:T(8,128)(2,1)S(1)}, u32[]{:S(2)}, u32[]{:S(2)}) collective-permute-start(bf16[832,256]{1,0:T(8,128)(2,1)S(1)} %get-tuple-element.80), channel_id=1, source_target_pairs={{0,8},{1,9},{2,10},{3,11},{4,12},{5,13},{6,14},{7,15},{8,0},{9,1},... | collective-permute-start | bytes 1277960 | tf_op jit(solution)/shard_map/ppermute | solution.py:395
  29.8 16.8 %collective-permute-start.2 = (bf16[832,256]{1,0:T(8,128)(2,1)S(1)}, bf16[832,256]{1,0:T(8,128)(2,1)S(1)}, u32[]{:S(2)}, u32[]{:S(2)}) collective-permute-start(bf16[832,256]{1,0:T(8,128)(2,1)S(1)} %get-tuple-element.81), channel_id=1, source_target_pairs={{0,12},{1,13},{2,14},{3,15},{4,0},{5,1},{6,2},{7,3},{8,4},{9,5},{1... | collective-permute-start | bytes 1277960 | tf_op jit(solution)/shard_map/ppermute | solution.py:395
  32.0 15.9 %collective-permute-start.3 = (bf16[832,256]{1,0:T(8,128)(2,1)S(1)}, bf16[832,256]{1,0:T(8,128)(2,1)S(1)}, u32[]{:S(2)}, u32[]{:S(2)}) collective-permute-start(bf16[832,256]{1,0:T(8,128)(2,1)S(1)} %get-tuple-element.83), channel_id=1, source_target_pairs={{0,1},{1,2},{2,3},{3,0},{4,5},{5,6},{6,7},{7,4},{8,9},{9,10},{10,1... | collective-permute-start | bytes 1277960 | tf_op jit(solution)/shard_map/ppermute | solution.py:395
  33.7 19.8 %collective-permute-start.4 = (bf16[832,256]{1,0:T(8,128)(2,1)S(1)}, bf16[832,256]{1,0:T(8,128)(2,1)S(1)}, u32[]{:S(2)}, u32[]{:S(2)}) collective-permute-start(bf16[832,256]{1,0:T(8,128)(2,1)S(1)} %get-tuple-element.84), channel_id=1, source_target_pairs={{0,2},{1,3},{2,0},{3,1},{4,6},{5,7},{6,4},{7,5},{8,10},{9,11},{10,... | collective-permute-start | bytes 1277960 | tf_op jit(solution)/shard_map/ppermute | solution.py:395
  36.9 23.7 %collective-permute-start.5 = (bf16[832,256]{1,0:T(8,128)(2,1)S(1)}, bf16[832,256]{1,0:T(8,128)(2,1)S(1)}, u32[]{:S(2)}, u32[]{:S(2)}) collective-permute-start(bf16[832,256]{1,0:T(8,128)(2,1)S(1)} %get-tuple-element.85), channel_id=1, source_target_pairs={{0,3},{1,0},{2,1},{3,2},{4,7},{5,4},{6,5},{7,6},{8,11},{9,8},{10,9... | collective-permute-start | bytes 1277960 | tf_op jit(solution)/shard_map/ppermute | solution.py:395
  45.5 19.3 %collective-permute-start.18 = (bf16[640,256]{1,0:T(8,128)(2,1)S(1)}, bf16[640,256]{1,0:T(8,128)(2,1)S(1)}, u32[]{:S(2)}, u32[]{:S(2)}) collective-permute-start(bf16[640,256]{1,0:T(8,128)(2,1)S(1)} %get-tuple-element.103), channel_id=1, source_target_pairs={{0,1},{1,2},{2,3},{3,0},{4,5},{5,6},{6,7},{7,4},{8,9},{9,10},{10,1... | collective-permute-start | bytes 983048 | tf_op jit(solution)/shard_map/ppermute | solution.py:395
  46.6 19.7 %collective-permute-start.19 = (bf16[640,256]{1,0:T(8,128)(2,1)S(1)}, bf16[640,256]{1,0:T(8,128)(2,1)S(1)}, u32[]{:S(2)}, u32[]{:S(2)}) collective-permute-start(bf16[640,256]{1,0:T(8,128)(2,1)S(1)} %get-tuple-element.104), channel_id=1, source_target_pairs={{0,2},{1,3},{2,0},{3,1},{4,6},{5,7},{6,4},{7,5},{8,10},{9,11},{10,... | collective-permute-start | bytes 983048 | tf_op jit(solution)/shard_map/ppermute | solution.py:395
  48.0 18.4 %collective-permute-start.20 = (bf16[640,256]{1,0:T(8,128)(2,1)S(1)}, bf16[640,256]{1,0:T(8,128)(2,1)S(1)}, u32[]{:S(2)}, u32[]{:S(2)}) collective-permute-start(bf16[640,256]{1,0:T(8,128)(2,1)S(1)} %get-tuple-element.105), channel_id=1, source_target_pairs={{0,3},{1,0},{2,1},{3,2},{4,7},{5,4},{6,5},{7,6},{8,11},{9,8},{10,9... | collective-permute-start | bytes 983048 | tf_op jit(solution)/shard_map/ppermute | solution.py:395
  53.4 16.6 %collective-permute-start.21 = (bf16[640,256]{1,0:T(8,128)(2,1)S(1)}, bf16[640,256]{1,0:T(8,128)(2,1)S(1)}, u32[]{:S(2)}, u32[]{:S(2)}) collective-permute-start(bf16[640,256]{1,0:T(8,128)(2,1)S(1)} %get-tuple-element.107), channel_id=1, source_target_pairs={{0,4},{1,5},{2,6},{3,7},{4,8},{5,9},{6,10},{7,11},{8,12},{9,13},{1... | collective-permute-start | bytes 983048 | tf_op jit(solution)/shard_map/ppermute | solution.py:395
  66.3 17.6 %collective-permute-start.7 = (bf16[640,256]{1,0:T(8,128)(2,1)S(1)}, bf16[640,256]{1,0:T(8,128)(2,1)S(1)}, u32[]{:S(2)}, u32[]{:S(2)}) collective-permute-start(bf16[640,256]{1,0:T(8,128)(2,1)S(1)} %get-tuple-element.88), channel_id=1, source_target_pairs={{0,2},{1,3},{2,0},{3,1},{4,6},{5,7},{6,4},{7,5},{8,10},{9,11},{10,... | collective-permute-start | bytes 983048 | tf_op jit(solution)/shard_map/ppermute | solution.py:395
  70.1 14.7 %collective-permute-start.8 = (bf16[640,256]{1,0:T(8,128)(2,1)S(1)}, bf16[640,256]{1,0:T(8,128)(2,1)S(1)}, u32[]{:S(2)}, u32[]{:S(2)}) collective-permute-start(bf16[640,256]{1,0:T(8,128)(2,1)S(1)} %get-tuple-element.89), channel_id=1, source_target_pairs={{0,3},{1,0},{2,1},{3,2},{4,7},{5,4},{6,5},{7,6},{8,11},{9,8},{10,9... | collective-permute-start | bytes 983048 | tf_op jit(solution)/shard_map/ppermute | solution.py:395
  72.7 18.3 %collective-permute-start.9 = (bf16[640,256]{1,0:T(8,128)(2,1)S(1)}, bf16[640,256]{1,0:T(8,128)(2,1)S(1)}, u32[]{:S(2)}, u32[]{:S(2)}) collective-permute-start(bf16[640,256]{1,0:T(8,128)(2,1)S(1)} %get-tuple-element.91), channel_id=1, source_target_pairs={{0,4},{1,5},{2,6},{3,7},{4,8},{5,9},{6,10},{7,11},{8,12},{9,13},{1... | collective-permute-start | bytes 983048 | tf_op jit(solution)/shard_map/ppermute | solution.py:395
  72.7 20.8 %collective-permute-start.10 = (bf16[640,256]{1,0:T(8,128)(2,1)S(1)}, bf16[640,256]{1,0:T(8,128)(2,1)S(1)}, u32[]{:S(2)}, u32[]{:S(2)}) collective-permute-start(bf16[640,256]{1,0:T(8,128)(2,1)S(1)} %get-tuple-element.92), channel_id=1, source_target_pairs={{0,8},{1,9},{2,10},{3,11},{4,12},{5,13},{6,14},{7,15},{8,0},{9,1},... | collective-permute-start | bytes 983048 | tf_op jit(solution)/shard_map/ppermute | solution.py:395
  75.5 19.2 %collective-permute-start.11 = (bf16[640,256]{1,0:T(8,128)(2,1)S(1)}, bf16[640,256]{1,0:T(8,128)(2,1)S(1)}, u32[]{:S(2)}, u32[]{:S(2)}) collective-permute-start(bf16[640,256]{1,0:T(8,128)(2,1)S(1)} %get-tuple-element.93), channel_id=1, source_target_pairs={{0,12},{1,13},{2,14},{3,15},{4,0},{5,1},{6,2},{7,3},{8,4},{9,5},{1... | collective-permute-start | bytes 983048 | tf_op jit(solution)/shard_map/ppermute | solution.py:395
  84.8 20.6 %collective-permute-start.35 = (bf16[576,256]{1,0:T(8,128)(2,1)S(1)}, bf16[576,256]{1,0:T(8,128)(2,1)S(1)}, u32[]{:S(2)}, u32[]{:S(2)}) collective-permute-start(bf16[576,256]{1,0:T(8,128)(2,1)S(1)} %get-tuple-element.132), channel_id=1, source_target_pairs={{0,2},{1,3},{2,0},{3,1},{4,6},{5,7},{6,4},{7,5},{8,10},{9,11},{10,... | collective-permute-start | bytes 884744 | tf_op jit(solution)/shard_map/ppermute | solution.py:395
  91.0 14.5 %collective-permute-start.36 = (bf16[576,256]{1,0:T(8,128)(2,1)S(1)}, bf16[576,256]{1,0:T(8,128)(2,1)S(1)}, u32[]{:S(2)}, u32[]{:S(2)}) collective-permute-start(bf16[576,256]{1,0:T(8,128)(2,1)S(1)} %get-tuple-element.133), channel_id=1, source_target_pairs={{0,1},{1,2},{2,3},{3,0},{4,5},{5,6},{6,7},{7,4},{8,9},{9,10},{10,1... | collective-permute-start | bytes 884744 | tf_op jit(solution)/shard_map/ppermute | solution.py:395
  109.4 29.5 %collective-permute-start.40 = (bf16[768,256]{1,0:T(8,128)(2,1)S(1)}, bf16[768,256]{1,0:T(8,128)(2,1)S(1)}, u32[]{:S(2)}, u32[]{:S(2)}) collective-permute-start(bf16[768,256]{1,0:T(8,128)(2,1)S(1)} %get-tuple-element.138), channel_id=1, source_target_pairs={{0,12},{1,13},{2,14},{3,15},{4,0},{5,1},{6,2},{7,3},{8,4},{9,5},{1... | collective-permute-start | bytes 1179656 | tf_op jit(solution)/shard_map/ppermute | solution.py:395
  111.7 27.3 %collective-permute-start.41 = (bf16[768,256]{1,0:T(8,128)(2,1)S(1)}, bf16[768,256]{1,0:T(8,128)(2,1)S(1)}, u32[]{:S(2)}, u32[]{:S(2)}) collective-permute-start(bf16[768,256]{1,0:T(8,128)(2,1)S(1)} %get-tuple-element.139), channel_id=1, source_target_pairs={{0,3},{1,0},{2,1},{3,2},{4,7},{5,4},{6,5},{7,6},{8,11},{9,8},{10,9... | collective-permute-start | bytes 1179656 | tf_op jit(solution)/shard_map/ppermute | solution.py:395
  112.8 16.0 %collective-permute-start.27 = (bf16[576,256]{1,0:T(8,128)(2,1)S(1)}, bf16[576,256]{1,0:T(8,128)(2,1)S(1)}, u32[]{:S(2)}, u32[]{:S(2)}) collective-permute-start(bf16[576,256]{1,0:T(8,128)(2,1)S(1)} %get-tuple-element.124), channel_id=1, source_target_pairs={{0,12},{1,13},{2,14},{3,15},{4,0},{5,1},{6,2},{7,3},{8,4},{9,5},{1... | collective-permute-start | bytes 884744 | tf_op jit(solution)/shard_map/ppermute | solution.py:395
  119.0 19.7 %collective-permute-start.29 = (bf16[576,256]{1,0:T(8,128)(2,1)S(1)}, bf16[576,256]{1,0:T(8,128)(2,1)S(1)}, u32[]{:S(2)}, u32[]{:S(2)}) collective-permute-start(bf16[576,256]{1,0:T(8,128)(2,1)S(1)} %get-tuple-element.126), channel_id=1, source_target_pairs={{0,4},{1,5},{2,6},{3,7},{4,8},{5,9},{6,10},{7,11},{8,12},{9,13},{1... | collective-permute-start | bytes 884744 | tf_op jit(solution)/shard_map/ppermute | solution.py:395
  128.8 17.9 %collective-permute-start.43 = (bf16[768,256]{1,0:T(8,128)(2,1)S(1)}, bf16[768,256]{1,0:T(8,128)(2,1)S(1)}, u32[]{:S(2)}, u32[]{:S(2)}) collective-permute-start(bf16[768,256]{1,0:T(8,128)(2,1)S(1)} %get-tuple-element.141), channel_id=1, source_target_pairs={{0,1},{1,2},{2,3},{3,0},{4,5},{5,6},{6,7},{7,4},{8,9},{9,10},{10,1... | collective-permute-start | bytes 1179656 | tf_op jit(solution)/shard_map/ppermute | solution.py:395
  138.7 22.5 %collective-permute-start.46 = (bf16[768,256]{1,0:T(8,128)(2,1)S(1)}, bf16[768,256]{1,0:T(8,128)(2,1)S(1)}, u32[]{:S(2)}, u32[]{:S(2)}) collective-permute-start(bf16[768,256]{1,0:T(8,128)(2,1)S(1)} %get-tuple-element.148), channel_id=1, source_target_pairs={{0,8},{1,9},{2,10},{3,11},{4,12},{5,13},{6,14},{7,15},{8,0},{9,1},... | collective-permute-start | bytes 1179656 | tf_op jit(solution)/shard_map/ppermute | solution.py:395
  138.9 22.3 %collective-permute-start.47 = (bf16[768,256]{1,0:T(8,128)(2,1)S(1)}, bf16[768,256]{1,0:T(8,128)(2,1)S(1)}, u32[]{:S(2)}, u32[]{:S(2)}) collective-permute-start(bf16[768,256]{1,0:T(8,128)(2,1)S(1)} %get-tuple-element.149), channel_id=1, source_target_pairs={{0,2},{1,3},{2,0},{3,1},{4,6},{5,7},{6,4},{7,5},{8,10},{9,11},{10,... | collective-permute-start | bytes 1179656 | tf_op jit(solution)/shard_map/ppermute | solution.py:395
  139.0 22.3 %collective-permute-start.44 = (bf16[768,256]{1,0:T(8,128)(2,1)S(1)}, bf16[768,256]{1,0:T(8,128)(2,1)S(1)}, u32[]{:S(2)}, u32[]{:S(2)}) collective-permute-start(bf16[768,256]{1,0:T(8,128)(2,1)S(1)} %get-tuple-element.144), channel_id=1, source_target_pairs={{0,8},{1,9},{2,10},{3,11},{4,12},{5,13},{6,14},{7,15},{8,0},{9,1},... | collective-permute-start | bytes 1179656 | tf_op jit(solution)/shard_map/ppermute | solution.py:395
  142.6 23.8 %collective-permute-start.45 = (bf16[768,256]{1,0:T(8,128)(2,1)S(1)}, bf16[768,256]{1,0:T(8,128)(2,1)S(1)}, u32[]{:S(2)}, u32[]{:S(2)}) collective-permute-start(bf16[768,256]{1,0:T(8,128)(2,1)S(1)} %get-tuple-element.145), channel_id=1, source_target_pairs={{0,2},{1,3},{2,0},{3,1},{4,6},{5,7},{6,4},{7,5},{8,10},{9,11},{10,... | collective-permute-start | bytes 1179656 | tf_op jit(solution)/shard_map/ppermute | solution.py:395
  146.8 23.8 %collective-permute-start.30 = (bf16[768,256]{1,0:T(8,128)(2,1)S(1)}, bf16[768,256]{1,0:T(8,128)(2,1)S(1)}, u32[]{:S(2)}, u32[]{:S(2)}) collective-permute-start(bf16[768,256]{1,0:T(8,128)(2,1)S(1)} %get-tuple-element.127), channel_id=1, source_target_pairs={{0,12},{1,13},{2,14},{3,15},{4,0},{5,1},{6,2},{7,3},{8,4},{9,5},{1... | collective-permute-start | bytes 1179656 | tf_op jit(solution)/shard_map/ppermute | solution.py:395
  (22 other events, 272.8 us)

commit v3 on v2

--- a/solution.py
+++ b/solution.py
@@ -206,7 +206,7 @@
     place = position()
     keep = 1.0 - residual_weight * refresh[chunk * PER_CHUNK + plus(place, 0, 0)].astype(f32)
     proj = [added([ref[SIDE * PACK : MIX] for ref in q]) for q in (q_left, q_right)]
-    near = [(keep * part.astype(f32)).astype(bf16) for part in proj]
+    near = (keep * jnp.concatenate(proj, axis=1).astype(f32)).astype(bf16)
     for k in range(SIDE):
         b_left[k][SIDE * ROWS : BACK] = proj[0]
         b_right[k][SIDE * ROWS : BACK] = proj[1]
@@ -216,10 +216,10 @@
         pieces = []
         for ref, at in ((q_left[dz], dx * PACK), (q_right[dx], dz * PACK)):
             pieces += [ref[at + ROWS : at + PACK, :128], ref[at + ROWS : at + PACK, 128:]]
-        bt = jnp.concatenate(pieces, axis=0)
+        low = mm_t(jnp.concatenate(pieces, axis=0), near)
         for side, ref, at in ((0, q_left[dz], dx * PACK), (1, q_right[dx], dz * PACK)):
-            value = ref[at : at + ROWS].astype(f32) + mm_t(bt, near[side])
-            m[i * ROWS : (i + 1) * ROWS, side * HALF : (side + 1) * HALF] = value.astype(bf16)
+            cols = slice(side * HALF, (side + 1) * HALF)
+            m[i * ROWS : (i + 1) * ROWS, cols] = (ref[at : at + ROWS].astype(f32) + low[:, cols]).astype(bf16)
 
     acc[...] = mm_t(m[:1024], m[:1024])
     acc[...] += mm_t(m[1024:], m[1024:])
@@ -231,7 +231,8 @@
     for block in blocks:
         trace += jnp.where(diagonal, acc[block, block], 0.0)
     inverse = 1.0 / (jnp.sqrt(jnp.sum(trace, axis=(0, 1), keepdims=True)) + epsilon)
-    gram[...] = (acc[...] * (inverse * inverse)).astype(bf16)
+    for block in blocks:
+        gram[block, :] = (acc[block, :] * (inverse * inverse)).astype(bf16)
 
     def factor(out):
         for at in range(0, FF, HALF):
@@ -255,12 +256,16 @@
     factor(f_one)
     f_two[...] = (inverse * mm(work[...], f_one[...])).astype(bf16)
 
-    for dx in range(SIDE):
-        value = mm(m[dx * 512 : (dx + 1) * 512, :], f_two[...]).astype(bf16)
-        for dz in range(SIDE):
-            rows = slice(dz * ROWS, (dz + 1) * ROWS)
-            b_left[dz][dx * ROWS : (dx + 1) * ROWS] = value[rows, :HALF]
-            b_right[dx][dz * ROWS : (dz + 1) * ROWS] = value[rows, HALF:]
+    for side in (0, 1):
+        right = f_two[:, side * HALF : (side + 1) * HALF]
+        for dx in range(SIDE):
+            value = mm(m[dx * 512 : (dx + 1) * 512, :], right).astype(bf16)
+            for dz in range(SIDE):
+                piece = value[dz * ROWS : (dz + 1) * ROWS]
+                if side == 0:
+                    b_left[dz][dx * ROWS : (dx + 1) * ROWS] = piece
+                else:
+                    b_right[dx][dz * ROWS : (dz + 1) * ROWS] = piece
 
 
 def orthogonalize(chunk, refresh, got):
@@ -435,8 +440,8 @@
         turned = turn(got_z + got_x)
         last.append(exchange(turned[:SIDE], turned[SIDE:], -1))
     outs = finish(((0, 0), (0, 2)), False, *state, weights, last, [])
-    outs = finish(((0, 1), (0, 3), (1, 0), (1, 2)), True, *state, weights, last, outs)
-    outs = finish(((1, 1), (1, 3)), True, *state, weights, last, outs)
+    outs = finish(((0, 1), (0, 3), (1, 0), (1, 2), (1, 1)), True, *state, weights, last, outs)
+    outs = finish(((1, 3),), True, *state, weights, last, outs)
     return tuple(outs)
 
 

time: 176 us -> 176 us (level); the launches traced: 173 us -> 176 us
  waiting for transfers between devices: 35.6 us -> 37.8 us
    ppermute x48, waiting for transfers between devices: 35.6 us -> 37.8 us  [send(): return lax.ppermute(array, 'row', pairs)]
  transfers between devices with their start and end apart: 48 -> 48, of which waited for: 12 -> 13; matrix products, arithmetic and copies ran while one was open for 0% -> 0% of each run, Pallas kernels for 16% -> 16%
where the time goes in v3:
time: 176 us
  starting transfers between devices  102 us (58%)
  waiting for transfers between devices  37.8 us (21%)
  Pallas kernels  34.7 us (20%)
    ppermute x48, starting transfers between devices, send(): return lax.ppermute(array, 'row', pairs)  102 us
    ppermute x48, waiting for transfers between devices, send(): return lax.ppermute(array, 'row', pairs)  37.8 us
    pallas_call x2, Pallas kernels, orthogonalize(): call(functools.partial(ortho_kernel, chunk), [shape(BACK, HALF)] * (2 * S...  13.3 us
    pallas_call x3, Pallas kernels, pack(): call(functools.partial(pack_kernel, chunk, steps), [shape(SIDE * FULL, HA...  10.8 us
    pallas_call x3, Pallas kernels, finish(): call(functools.partial(finish_kernel, parts, unroll, count), [shape(CHUNK...  9.68 us
  transfers between devices with their start and end apart: 48, of which 13 were waited for; matrix products, arithmetic and copies ran while one was open for 0% of the time, Pallas kernels for 16%

profile of v3, /device:TPU:64, one launch (start us, length us, event | category | flops | bytes accessed | tf_op | source)
XLA Modules:
  0.0 175.9 jit_solution(14803277864447386752)
XLA Ops:
  0.7 3.7 %shard_map.80 = (bf16[832,256]{1,0:T(8,128)(2,1)S(1)}, bf16[832,256]{1,0:T(8,128)(2,1)S(1)}) custom-call(s32[1,32]{1,0:T(1,128)} %chosen.5, s32[32]{0:T(128)} %refresh.9, bf16[32,128,512]{2,1,0:T(8,128)(2,1)} %grads.11, bf16[32,128,512]{2,1,0:T(8,128)(2,1)} %bank.11, f32[32,64,128]{2,1,0:T(8,128)} %bitcast.1), custom_call_target="tpu_custom_call" | custom-call | flops 100000000 | bytes 3000000 | tf_op jit(solution)/shard_map/pallas_call | solution.py:156
  4.4 3.1 %collective-permute-start.13 = (bf16[832,256]{1,0:T(8,128)(2,1)S(1)}, bf16[832,256]{1,0:T(8,128)(2,1)S(1)}, u32[]{:S(2)}, u32[]{:S(2)}) collective-permute-start(bf16[832,256]{1,0:T(8,128)(2,1)S(1)} %get-tuple-element.96), channel_id=1, source_target_pairs={{0,8},{1,9},{2,10},{3,11},{4,12},{5,13},{6,14},{7,15},{8,0},{9,1},... | collective-permute-start | bytes 1277960 | tf_op jit(solution)/shard_map/ppermute | solution.py:400
  7.5 3.3 %shard_map.79 = (bf16[832,256]{1,0:T(8,128)(2,1)S(1)}, bf16[832,256]{1,0:T(8,128)(2,1)S(1)}, bf16[832,256]{1,0:T(8,128)(2,1)S(1)}, bf16[832,256]{1,0:T(8,128)(2,...) custom-call(s32[1,32]{1,0:T(1,128)S(1)} %copy-done.4, s32[32]{0:T(128)S(1)} %copy-done.5, ...), custom_call_target="tpu_custom_call" | custom-call | flops 300000000 | bytes 9000000 | tf_op jit(solution)/shard_map/pallas_call | solution.py:156
  11.5 2.6 %collective-permute-start.14 = (bf16[832,256]{1,0:T(8,128)(2,1)S(1)}, bf16[832,256]{1,0:T(8,128)(2,1)S(1)}, u32[]{:S(2)}, u32[]{:S(2)}) collective-permute-start(bf16[832,256]{1,0:T(8,128)(2,1)S(1)} %get-tuple-element.97), channel_id=1, source_target_pairs={{0,12},{1,13},{2,14},{3,15},{4,0},{5,1},{6,2},{7,3},{8,4},{9,5},{1... | collective-permute-start | bytes 1277960 | tf_op jit(solution)/shard_map/ppermute | solution.py:400
  14.1 2.2 %collective-permute-start.15 = (bf16[832,256]{1,0:T(8,128)(2,1)S(1)}, bf16[832,256]{1,0:T(8,128)(2,1)S(1)}, u32[]{:S(2)}, u32[]{:S(2)}) collective-permute-start(bf16[832,256]{1,0:T(8,128)(2,1)S(1)} %get-tuple-element.99), channel_id=1, source_target_pairs={{0,1},{1,2},{2,3},{3,0},{4,5},{5,6},{6,7},{7,4},{8,9},{9,10},{10,1... | collective-permute-start | bytes 1277960 | tf_op jit(solution)/shard_map/ppermute | solution.py:400
  16.3 3.9 %shard_map.77 = (bf16[832,256]{1,0:T(8,128)(2,1)S(1)}, bf16[832,256]{1,0:T(8,128)(2,1)S(1)}, bf16[832,256]{1,0:T(8,128)(2,1)S(1)}, bf16[832,256]{1,0:T(8,128)(2,...) custom-call(s32[1,32]{1,0:T(1,128)S(1)} %copy-done.4, ...), custom_call_target="tpu_custom_call" | custom-call | flops 400000000 | bytes 12000000 | tf_op jit(solution)/shard_map/pallas_call | solution.py:156
  22.3 4.5 %collective-permute-done.12.refs_1_ = bf16[832,256]{1,0:T(8,128)(2,1)S(1)} collective-permute-done((bf16[832,256]{1,0:T(8,128)(2,1)S(1)}, bf16[832,256]{1,0:T(8,128)(2,1)S(1)}, u32[]{:S(2)}, u32[]{:S(2)}) %collective-permute-start.12) | collective-permute-done | bytes 426016 | tf_op jit(solution)/shard_map/ppermute | solution.py:400
  26.9 2.9 %collective-permute-start.1 = (bf16[832,256]{1,0:T(8,128)(2,1)S(1)}, bf16[832,256]{1,0:T(8,128)(2,1)S(1)}, u32[]{:S(2)}, u32[]{:S(2)}) collective-permute-start(bf16[832,256]{1,0:T(8,128)(2,1)S(1)} %get-tuple-element.80), channel_id=1, source_target_pairs={{0,8},{1,9},{2,10},{3,11},{4,12},{5,13},{6,14},{7,15},{8,0},{9,1},... | collective-permute-start | bytes 1277960 | tf_op jit(solution)/shard_map/ppermute | solution.py:400
  29.8 2.2 %collective-permute-start.2 = (bf16[832,256]{1,0:T(8,128)(2,1)S(1)}, bf16[832,256]{1,0:T(8,128)(2,1)S(1)}, u32[]{:S(2)}, u32[]{:S(2)}) collective-permute-start(bf16[832,256]{1,0:T(8,128)(2,1)S(1)} %get-tuple-element.81), channel_id=1, source_target_pairs={{0,12},{1,13},{2,14},{3,15},{4,0},{5,1},{6,2},{7,3},{8,4},{9,5},{1... | collective-permute-start | bytes 1277960 | tf_op jit(solution)/shard_map/ppermute | solution.py:400
  33.7 3.2 %collective-permute-done.refs_1_ = bf16[832,256]{1,0:T(8,128)(2,1)S(1)} collective-permute-done((bf16[832,256]{1,0:T(8,128)(2,1)S(1)}, bf16[832,256]{1,0:T(8,128)(2,1)S(1)}, u32[]{:S(2)}, u32[]{:S(2)}) %collective-permute-start) | collective-permute-done | bytes 426016 | tf_op jit(solution)/shard_map/ppermute | solution.py:400
  36.9 8.4 %collective-permute-start.5 = (bf16[832,256]{1,0:T(8,128)(2,1)S(1)}, bf16[832,256]{1,0:T(8,128)(2,1)S(1)}, u32[]{:S(2)}, u32[]{:S(2)}) collective-permute-start(bf16[832,256]{1,0:T(8,128)(2,1)S(1)} %get-tuple-element.85), channel_id=1, source_target_pairs={{0,3},{1,0},{2,1},{3,2},{4,7},{5,4},{6,5},{7,6},{8,11},{9,8},{10,9... | collective-permute-start | bytes 1277960 | tf_op jit(solution)/shard_map/ppermute | solution.py:400
  49.4 4.0 %collective-permute-done.4.refs_6_ = bf16[832,256]{1,0:T(8,128)(2,1)S(1)} collective-permute-done((bf16[832,256]{1,0:T(8,128)(2,1)S(1)}, bf16[832,256]{1,0:T(8,128)(2,1)S(1)}, u32[]{:S(2)}, u32[]{:S(2)}) %collective-permute-start.4) | collective-permute-done | bytes 426016 | tf_op jit(solution)/shard_map/ppermute | solution.py:400
  53.6 6.9 %collective-permute-done.5.refs_7_ = bf16[832,256]{1,0:T(8,128)(2,1)S(1)} collective-permute-done((bf16[832,256]{1,0:T(8,128)(2,1)S(1)}, bf16[832,256]{1,0:T(8,128)(2,1)S(1)}, u32[]{:S(2)}, u32[]{:S(2)}) %collective-permute-start.5) | collective-permute-done | bytes 426016 | tf_op jit(solution)/shard_map/ppermute | solution.py:400
  60.8 4.0 %collective-permute-done.18.refs_1_ = bf16[640,256]{1,0:T(8,128)(2,1)S(1)} collective-permute-done((bf16[640,256]{1,0:T(8,128)(2,1)S(1)}, bf16[640,256]{1,0:T(8,128)(2,1)S(1)}, u32[]{:S(2)}, u32[]{:S(2)}) %collective-permute-start.18) | collective-permute-done | bytes 327712 | tf_op jit(solution)/shard_map/ppermute | solution.py:400
  66.3 3.7 %collective-permute-start.7 = (bf16[640,256]{1,0:T(8,128)(2,1)S(1)}, bf16[640,256]{1,0:T(8,128)(2,1)S(1)}, u32[]{:S(2)}, u32[]{:S(2)}) collective-permute-start(bf16[640,256]{1,0:T(8,128)(2,1)S(1)} %get-tuple-element.88), channel_id=1, source_target_pairs={{0,2},{1,3},{2,0},{3,1},{4,6},{5,7},{6,4},{7,5},{8,10},{9,11},{10,... | collective-permute-start | bytes 983048 | tf_op jit(solution)/shard_map/ppermute | solution.py:400
  70.1 2.6 %collective-permute-start.8 = (bf16[640,256]{1,0:T(8,128)(2,1)S(1)}, bf16[640,256]{1,0:T(8,128)(2,1)S(1)}, u32[]{:S(2)}, u32[]{:S(2)}) collective-permute-start(bf16[640,256]{1,0:T(8,128)(2,1)S(1)} %get-tuple-element.89), channel_id=1, source_target_pairs={{0,3},{1,0},{2,1},{3,2},{4,7},{5,4},{6,5},{7,6},{8,11},{9,8},{10,9... | collective-permute-start | bytes 983048 | tf_op jit(solution)/shard_map/ppermute | solution.py:400
  77.2 6.6 %shard_map.82 = (bf16[576,256]{1,0:T(8,128)(2,1)S(1)}, bf16[576,256]{1,0:T(8,128)(2,1)S(1)}, bf16[576,256]{1,0:T(8,128)(2,1)S(1)}, bf16[576,256]{1,0:T(8,128)(2,...) custom-call(s32[32]{0:T(128)S(1)} %copy-done.5, ...), custom_call_target="tpu_custom_call" | custom-call | flops 8000000000 | bytes 5000000 | tf_op jit(solution)/shard_map/pallas_call | solution.py:272
  84.7 6.2 %collective-permute-start.33 = (bf16[576,256]{1,0:T(8,128)(2,1)S(1)}, bf16[576,256]{1,0:T(8,128)(2,1)S(1)}, u32[]{:S(2)}, u32[]{:S(2)}) collective-permute-start(bf16[576,256]{1,0:T(8,128)(2,1)S(1)} %get-tuple-element.130), channel_id=1, source_target_pairs={{0,2},{1,3},{2,0},{3,1},{4,6},{5,7},{6,4},{7,5},{8,10},{9,11},{10,... | collective-permute-start | bytes 884744 | tf_op jit(solution)/shard_map/ppermute | solution.py:400
  90.9 2.5 %collective-permute-start.34 = (bf16[576,256]{1,0:T(8,128)(2,1)S(1)}, bf16[576,256]{1,0:T(8,128)(2,1)S(1)}, u32[]{:S(2)}, u32[]{:S(2)}) collective-permute-start(bf16[576,256]{1,0:T(8,128)(2,1)S(1)} %get-tuple-element.131), channel_id=1, source_target_pairs={{0,1},{1,2},{2,3},{3,0},{4,5},{5,6},{6,7},{7,4},{8,9},{9,10},{10,1... | collective-permute-start | bytes 884744 | tf_op jit(solution)/shard_map/ppermute | solution.py:400
  94.6 2.5 %collective-permute-start.36 = (bf16[576,256]{1,0:T(8,128)(2,1)S(1)}, bf16[576,256]{1,0:T(8,128)(2,1)S(1)}, u32[]{:S(2)}, u32[]{:S(2)}) collective-permute-start(bf16[576,256]{1,0:T(8,128)(2,1)S(1)} %get-tuple-element.134), channel_id=1, source_target_pairs={{0,8},{1,9},{2,10},{3,11},{4,12},{5,13},{6,14},{7,15},{8,0},{9,1},... | collective-permute-start | bytes 884744 | tf_op jit(solution)/shard_map/ppermute | solution.py:400
  98.5 6.7 %shard_map.83 = (bf16[576,256]{1,0:T(8,128)(2,1)S(1)}, bf16[576,256]{1,0:T(8,128)(2,1)S(1)}, bf16[576,256]{1,0:T(8,128)(2,1)S(1)}, bf16[576,256]{1,0:T(8,128)(2,...) custom-call(s32[32]{0:T(128)S(1)} %copy-done.5, ...), custom_call_target="tpu_custom_call" | custom-call | flops 8000000000 | bytes 5000000 | tf_op jit(solution)/shard_map/pallas_call | solution.py:272
  109.3 2.3 %collective-permute-start.38 = (bf16[768,256]{1,0:T(8,128)(2,1)S(1)}, bf16[768,256]{1,0:T(8,128)(2,1)S(1)}, u32[]{:S(2)}, u32[]{:S(2)}) collective-permute-start(bf16[768,256]{1,0:T(8,128)(2,1)S(1)} %get-tuple-element.136), channel_id=1, source_target_pairs={{0,12},{1,13},{2,14},{3,15},{4,0},{5,1},{6,2},{7,3},{8,4},{9,5},{1... | collective-permute-start | bytes 1179656 | tf_op jit(solution)/shard_map/ppermute | solution.py:400
  112.5 4.5 %collective-permute-start.27 = (bf16[576,256]{1,0:T(8,128)(2,1)S(1)}, bf16[576,256]{1,0:T(8,128)(2,1)S(1)}, u32[]{:S(2)}, u32[]{:S(2)}) collective-permute-start(bf16[576,256]{1,0:T(8,128)(2,1)S(1)} %get-tuple-element.124), channel_id=1, source_target_pairs={{0,12},{1,13},{2,14},{3,15},{4,0},{5,1},{6,2},{7,3},{8,4},{9,5},{1... | collective-permute-start | bytes 884744 | tf_op jit(solution)/shard_map/ppermute | solution.py:400
  119.9 8.7 %collective-permute-done.27.refs_5_ = bf16[576,256]{1,0:T(8,128)(2,1)S(1)} collective-permute-done((bf16[576,256]{1,0:T(8,128)(2,1)S(1)}, bf16[576,256]{1,0:T(8,128)(2,1)S(1)}, u32[]{:S(2)}, u32[]{:S(2)}) %collective-permute-start.27) | collective-permute-done | bytes 294944 | tf_op jit(solution)/shard_map/ppermute | solution.py:400
  128.6 9.9 %collective-permute-start.41 = (bf16[768,256]{1,0:T(8,128)(2,1)S(1)}, bf16[768,256]{1,0:T(8,128)(2,1)S(1)}, u32[]{:S(2)}, u32[]{:S(2)}) collective-permute-start(bf16[768,256]{1,0:T(8,128)(2,1)S(1)} %get-tuple-element.139), channel_id=1, source_target_pairs={{0,1},{1,2},{2,3},{3,0},{4,5},{5,6},{6,7},{7,4},{8,9},{9,10},{10,1... | collective-permute-start | bytes 1179656 | tf_op jit(solution)/shard_map/ppermute | solution.py:400
  138.8 3.6 %collective-permute-start.42 = (bf16[768,256]{1,0:T(8,128)(2,1)S(1)}, bf16[768,256]{1,0:T(8,128)(2,1)S(1)}, u32[]{:S(2)}, u32[]{:S(2)}) collective-permute-start(bf16[768,256]{1,0:T(8,128)(2,1)S(1)} %get-tuple-element.142), channel_id=1, source_target_pairs={{0,8},{1,9},{2,10},{3,11},{4,12},{5,13},{6,14},{7,15},{8,0},{9,1},... | collective-permute-start | bytes 1179656 | tf_op jit(solution)/shard_map/ppermute | solution.py:400
  142.5 3.7 %collective-permute-start.43 = (bf16[768,256]{1,0:T(8,128)(2,1)S(1)}, bf16[768,256]{1,0:T(8,128)(2,1)S(1)}, u32[]{:S(2)}, u32[]{:S(2)}) collective-permute-start(bf16[768,256]{1,0:T(8,128)(2,1)S(1)} %get-tuple-element.143), channel_id=1, source_target_pairs={{0,2},{1,3},{2,0},{3,1},{4,6},{5,7},{6,4},{7,5},{8,10},{9,11},{10,... | collective-permute-start | bytes 1179656 | tf_op jit(solution)/shard_map/ppermute | solution.py:400
  146.4 14.8 %collective-permute-start.44 = (bf16[768,256]{1,0:T(8,128)(2,1)S(1)}, bf16[768,256]{1,0:T(8,128)(2,1)S(1)}, u32[]{:S(2)}, u32[]{:S(2)}) collective-permute-start(bf16[768,256]{1,0:T(8,128)(2,1)S(1)} %get-tuple-element.144), channel_id=1, source_target_pairs={{0,12},{1,13},{2,14},{3,15},{4,0},{5,1},{6,2},{7,3},{8,4},{9,5},{1... | collective-permute-start | bytes 1179656 | tf_op jit(solution)/shard_map/ppermute | solution.py:400
  161.2 2.3 %collective-permute-start.31 = (bf16[768,256]{1,0:T(8,128)(2,1)S(1)}, bf16[768,256]{1,0:T(8,128)(2,1)S(1)}, u32[]{:S(2)}, u32[]{:S(2)}) collective-permute-start(bf16[768,256]{1,0:T(8,128)(2,1)S(1)} %get-tuple-element.128), channel_id=1, source_target_pairs={{0,1},{1,2},{2,3},{3,0},{4,5},{5,6},{6,7},{7,4},{8,9},{9,10},{10,1... | collective-permute-start | bytes 1179656 | tf_op jit(solution)/shard_map/ppermute | solution.py:400
  163.5 2.9 %shard_map.86 = (bf16[32,128,512]{2,1,0:T(8,128)(2,1)}, bf16[32,128,512]{2,1,0:T(8,128)(2,1)}) custom-call(s32[1,32]{1,0:T(1,128)S(1)} %copy-done.4, s32[32]{0:T(128)S(1)} %copy-done.5, bf16[32,128,512]{2,1,0:T(8,128)(2,1)S(1)} %copy-done, bf16[32,128,512]{2,1,0:T(8,128)(2,1)S(1)} %copy-done.1, f32[32,64,128]{2,1,0:T(8,128)S(1)} %bitcast.4, ...), custom_call_target="tpu_custom_call" | custom-call | flops 300000000 | bytes 5000000 | tf_op jit(solution)/shard_map/pallas_call | solution.py:376
  166.4 2.5 %collective-permute-done.45.refs_9_ = bf16[768,256]{1,0:T(8,128)(2,1)S(1)} collective-permute-done((bf16[768,256]{1,0:T(8,128)(2,1)S(1)}, bf16[768,256]{1,0:T(8,128)(2,1)S(1)}, u32[]{:S(2)}, u32[]{:S(2)}) %collective-permute-start.45) | collective-permute-done | bytes 393248 | tf_op jit(solution)/shard_map/ppermute | solution.py:400
  168.9 4.8 %shard_map.87 = (bf16[32,128,512]{2,1,0:T(8,128)(2,1)}, bf16[32,128,512]{2,1,0:T(8,128)(2,1)}) custom-call(s32[1,32]{1,0:T(1,128)S(1)} %copy-done.4, s32[32]{0:T(128)S(1)} %copy-done.5, bf16[32,128,512]{2,1,0:T(8,128)(2,1)S(1)} %copy-done, bf16[32,128,512]{2,1,0:T(8,128)(2,1)S(1)} %copy-done.1, ...), custom_call_target="tpu_custom_call", output_to_operand_aliasing={{0}: (16, {}), {1}: (17, {})} | custom-call | flops 750000000 | bytes 12500000 | tf_op jit(solution)/shard_map/pallas_call | solution.py:376
  (88 shorter events, 29.1 us)
Async XLA Ops:
  4.4 15.7 %collective-permute-start.13 = (bf16[832,256]{1,0:T(8,128)(2,1)S(1)}, bf16[832,256]{1,0:T(8,128)(2,1)S(1)}, u32[]{:S(2)}, u32[]{:S(2)}) collective-permute-start(bf16[832,256]{1,0:T(8,128)(2,1)S(1)} %get-tuple-element.96), channel_id=1, source_target_pairs={{0,8},{1,9},{2,10},{3,11},{4,12},{5,13},{6,14},{7,15},{8,0},{9,1},... | collective-permute-start | bytes 1277960 | tf_op jit(solution)/shard_map/ppermute | solution.py:400
  7.5 14.2 %collective-permute-start.16 = (bf16[832,256]{1,0:T(8,128)(2,1)S(1)}, bf16[832,256]{1,0:T(8,128)(2,1)S(1)}, u32[]{:S(2)}, u32[]{:S(2)}) collective-permute-start(bf16[832,256]{1,0:T(8,128)(2,1)S(1)} %get-tuple-element.100), channel_id=1, source_target_pairs={{0,2},{1,3},{2,0},{3,1},{4,6},{5,7},{6,4},{7,5},{8,10},{9,11},{10,... | collective-permute-start | bytes 1277960 | tf_op jit(solution)/shard_map/ppermute | solution.py:400
  10.8 16.1 %collective-permute-start.12 = (bf16[832,256]{1,0:T(8,128)(2,1)S(1)}, bf16[832,256]{1,0:T(8,128)(2,1)S(1)}, u32[]{:S(2)}, u32[]{:S(2)}) collective-permute-start(bf16[832,256]{1,0:T(8,128)(2,1)S(1)} %get-tuple-element.95), channel_id=1, source_target_pairs={{0,4},{1,5},{2,6},{3,7},{4,8},{5,9},{6,10},{7,11},{8,12},{9,13},{1... | collective-permute-start | bytes 1277960 | tf_op jit(solution)/shard_map/ppermute | solution.py:400
  11.5 18.3 %collective-permute-start.14 = (bf16[832,256]{1,0:T(8,128)(2,1)S(1)}, bf16[832,256]{1,0:T(8,128)(2,1)S(1)}, u32[]{:S(2)}, u32[]{:S(2)}) collective-permute-start(bf16[832,256]{1,0:T(8,128)(2,1)S(1)} %get-tuple-element.97), channel_id=1, source_target_pairs={{0,12},{1,13},{2,14},{3,15},{4,0},{5,1},{6,2},{7,3},{8,4},{9,5},{1... | collective-permute-start | bytes 1277960 | tf_op jit(solution)/shard_map/ppermute | solution.py:400
  14.1 17.9 %collective-permute-start.15 = (bf16[832,256]{1,0:T(8,128)(2,1)S(1)}, bf16[832,256]{1,0:T(8,128)(2,1)S(1)}, u32[]{:S(2)}, u32[]{:S(2)}) collective-permute-start(bf16[832,256]{1,0:T(8,128)(2,1)S(1)} %get-tuple-element.99), channel_id=1, source_target_pairs={{0,1},{1,2},{2,3},{3,0},{4,5},{5,6},{6,7},{7,4},{8,9},{9,10},{10,1... | collective-permute-start | bytes 1277960 | tf_op jit(solution)/shard_map/ppermute | solution.py:400
  21.7 15.1 %collective-permute-start = (bf16[832,256]{1,0:T(8,128)(2,1)S(1)}, bf16[832,256]{1,0:T(8,128)(2,1)S(1)}, u32[]{:S(2)}, u32[]{:S(2)}) collective-permute-start(bf16[832,256]{1,0:T(8,128)(2,1)S(1)} %get-tuple-element.79), channel_id=1, source_target_pairs={{0,4},{1,5},{2,6},{3,7},{4,8},{5,9},{6,10},{7,11},{8,12},{9,13},{1... | collective-permute-start | bytes 1277960 | tf_op jit(solution)/shard_map/ppermute | solution.py:400
  26.9 18.6 %collective-permute-start.1 = (bf16[832,256]{1,0:T(8,128)(2,1)S(1)}, bf16[832,256]{1,0:T(8,128)(2,1)S(1)}, u32[]{:S(2)}, u32[]{:S(2)}) collective-permute-start(bf16[832,256]{1,0:T(8,128)(2,1)S(1)} %get-tuple-element.80), channel_id=1, source_target_pairs={{0,8},{1,9},{2,10},{3,11},{4,12},{5,13},{6,14},{7,15},{8,0},{9,1},... | collective-permute-start | bytes 1277960 | tf_op jit(solution)/shard_map/ppermute | solution.py:400
  29.8 16.8 %collective-permute-start.2 = (bf16[832,256]{1,0:T(8,128)(2,1)S(1)}, bf16[832,256]{1,0:T(8,128)(2,1)S(1)}, u32[]{:S(2)}, u32[]{:S(2)}) collective-permute-start(bf16[832,256]{1,0:T(8,128)(2,1)S(1)} %get-tuple-element.81), channel_id=1, source_target_pairs={{0,12},{1,13},{2,14},{3,15},{4,0},{5,1},{6,2},{7,3},{8,4},{9,5},{1... | collective-permute-start | bytes 1277960 | tf_op jit(solution)/shard_map/ppermute | solution.py:400
  32.0 15.9 %collective-permute-start.3 = (bf16[832,256]{1,0:T(8,128)(2,1)S(1)}, bf16[832,256]{1,0:T(8,128)(2,1)S(1)}, u32[]{:S(2)}, u32[]{:S(2)}) collective-permute-start(bf16[832,256]{1,0:T(8,128)(2,1)S(1)} %get-tuple-element.83), channel_id=1, source_target_pairs={{0,1},{1,2},{2,3},{3,0},{4,5},{5,6},{6,7},{7,4},{8,9},{9,10},{10,1... | collective-permute-start | bytes 1277960 | tf_op jit(solution)/shard_map/ppermute | solution.py:400
  33.7 19.8 %collective-permute-start.4 = (bf16[832,256]{1,0:T(8,128)(2,1)S(1)}, bf16[832,256]{1,0:T(8,128)(2,1)S(1)}, u32[]{:S(2)}, u32[]{:S(2)}) collective-permute-start(bf16[832,256]{1,0:T(8,128)(2,1)S(1)} %get-tuple-element.84), channel_id=1, source_target_pairs={{0,2},{1,3},{2,0},{3,1},{4,6},{5,7},{6,4},{7,5},{8,10},{9,11},{10,... | collective-permute-start | bytes 1277960 | tf_op jit(solution)/shard_map/ppermute | solution.py:400
  36.9 23.7 %collective-permute-start.5 = (bf16[832,256]{1,0:T(8,128)(2,1)S(1)}, bf16[832,256]{1,0:T(8,128)(2,1)S(1)}, u32[]{:S(2)}, u32[]{:S(2)}) collective-permute-start(bf16[832,256]{1,0:T(8,128)(2,1)S(1)} %get-tuple-element.85), channel_id=1, source_target_pairs={{0,3},{1,0},{2,1},{3,2},{4,7},{5,4},{6,5},{7,6},{8,11},{9,8},{10,9... | collective-permute-start | bytes 1277960 | tf_op jit(solution)/shard_map/ppermute | solution.py:400
  45.5 19.3 %collective-permute-start.18 = (bf16[640,256]{1,0:T(8,128)(2,1)S(1)}, bf16[640,256]{1,0:T(8,128)(2,1)S(1)}, u32[]{:S(2)}, u32[]{:S(2)}) collective-permute-start(bf16[640,256]{1,0:T(8,128)(2,1)S(1)} %get-tuple-element.103), channel_id=1, source_target_pairs={{0,1},{1,2},{2,3},{3,0},{4,5},{5,6},{6,7},{7,4},{8,9},{9,10},{10,1... | collective-permute-start | bytes 983048 | tf_op jit(solution)/shard_map/ppermute | solution.py:400
  46.6 19.7 %collective-permute-start.19 = (bf16[640,256]{1,0:T(8,128)(2,1)S(1)}, bf16[640,256]{1,0:T(8,128)(2,1)S(1)}, u32[]{:S(2)}, u32[]{:S(2)}) collective-permute-start(bf16[640,256]{1,0:T(8,128)(2,1)S(1)} %get-tuple-element.104), channel_id=1, source_target_pairs={{0,2},{1,3},{2,0},{3,1},{4,6},{5,7},{6,4},{7,5},{8,10},{9,11},{10,... | collective-permute-start | bytes 983048 | tf_op jit(solution)/shard_map/ppermute | solution.py:400
  48.0 18.4 %collective-permute-start.20 = (bf16[640,256]{1,0:T(8,128)(2,1)S(1)}, bf16[640,256]{1,0:T(8,128)(2,1)S(1)}, u32[]{:S(2)}, u32[]{:S(2)}) collective-permute-start(bf16[640,256]{1,0:T(8,128)(2,1)S(1)} %get-tuple-element.105), channel_id=1, source_target_pairs={{0,3},{1,0},{2,1},{3,2},{4,7},{5,4},{6,5},{7,6},{8,11},{9,8},{10,9... | collective-permute-start | bytes 983048 | tf_op jit(solution)/shard_map/ppermute | solution.py:400
  53.4 16.6 %collective-permute-start.21 = (bf16[640,256]{1,0:T(8,128)(2,1)S(1)}, bf16[640,256]{1,0:T(8,128)(2,1)S(1)}, u32[]{:S(2)}, u32[]{:S(2)}) collective-permute-start(bf16[640,256]{1,0:T(8,128)(2,1)S(1)} %get-tuple-element.107), channel_id=1, source_target_pairs={{0,4},{1,5},{2,6},{3,7},{4,8},{5,9},{6,10},{7,11},{8,12},{9,13},{1... | collective-permute-start | bytes 983048 | tf_op jit(solution)/shard_map/ppermute | solution.py:400
  66.3 17.5 %collective-permute-start.7 = (bf16[640,256]{1,0:T(8,128)(2,1)S(1)}, bf16[640,256]{1,0:T(8,128)(2,1)S(1)}, u32[]{:S(2)}, u32[]{:S(2)}) collective-permute-start(bf16[640,256]{1,0:T(8,128)(2,1)S(1)} %get-tuple-element.88), channel_id=1, source_target_pairs={{0,2},{1,3},{2,0},{3,1},{4,6},{5,7},{6,4},{7,5},{8,10},{9,11},{10,... | collective-permute-start | bytes 983048 | tf_op jit(solution)/shard_map/ppermute | solution.py:400
  70.1 14.6 %collective-permute-start.8 = (bf16[640,256]{1,0:T(8,128)(2,1)S(1)}, bf16[640,256]{1,0:T(8,128)(2,1)S(1)}, u32[]{:S(2)}, u32[]{:S(2)}) collective-permute-start(bf16[640,256]{1,0:T(8,128)(2,1)S(1)} %get-tuple-element.89), channel_id=1, source_target_pairs={{0,3},{1,0},{2,1},{3,2},{4,7},{5,4},{6,5},{7,6},{8,11},{9,8},{10,9... | collective-permute-start | bytes 983048 | tf_op jit(solution)/shard_map/ppermute | solution.py:400
  72.7 18.2 %collective-permute-start.9 = (bf16[640,256]{1,0:T(8,128)(2,1)S(1)}, bf16[640,256]{1,0:T(8,128)(2,1)S(1)}, u32[]{:S(2)}, u32[]{:S(2)}) collective-permute-start(bf16[640,256]{1,0:T(8,128)(2,1)S(1)} %get-tuple-element.91), channel_id=1, source_target_pairs={{0,4},{1,5},{2,6},{3,7},{4,8},{5,9},{6,10},{7,11},{8,12},{9,13},{1... | collective-permute-start | bytes 983048 | tf_op jit(solution)/shard_map/ppermute | solution.py:400
  72.7 20.7 %collective-permute-start.10 = (bf16[640,256]{1,0:T(8,128)(2,1)S(1)}, bf16[640,256]{1,0:T(8,128)(2,1)S(1)}, u32[]{:S(2)}, u32[]{:S(2)}) collective-permute-start(bf16[640,256]{1,0:T(8,128)(2,1)S(1)} %get-tuple-element.92), channel_id=1, source_target_pairs={{0,8},{1,9},{2,10},{3,11},{4,12},{5,13},{6,14},{7,15},{8,0},{9,1},... | collective-permute-start | bytes 983048 | tf_op jit(solution)/shard_map/ppermute | solution.py:400
  75.5 19.1 %collective-permute-start.11 = (bf16[640,256]{1,0:T(8,128)(2,1)S(1)}, bf16[640,256]{1,0:T(8,128)(2,1)S(1)}, u32[]{:S(2)}, u32[]{:S(2)}) collective-permute-start(bf16[640,256]{1,0:T(8,128)(2,1)S(1)} %get-tuple-element.93), channel_id=1, source_target_pairs={{0,12},{1,13},{2,14},{3,15},{4,0},{5,1},{6,2},{7,3},{8,4},{9,5},{1... | collective-permute-start | bytes 983048 | tf_op jit(solution)/shard_map/ppermute | solution.py:400
  84.7 20.5 %collective-permute-start.33 = (bf16[576,256]{1,0:T(8,128)(2,1)S(1)}, bf16[576,256]{1,0:T(8,128)(2,1)S(1)}, u32[]{:S(2)}, u32[]{:S(2)}) collective-permute-start(bf16[576,256]{1,0:T(8,128)(2,1)S(1)} %get-tuple-element.130), channel_id=1, source_target_pairs={{0,2},{1,3},{2,0},{3,1},{4,6},{5,7},{6,4},{7,5},{8,10},{9,11},{10,... | collective-permute-start | bytes 884744 | tf_op jit(solution)/shard_map/ppermute | solution.py:400
  90.9 14.4 %collective-permute-start.34 = (bf16[576,256]{1,0:T(8,128)(2,1)S(1)}, bf16[576,256]{1,0:T(8,128)(2,1)S(1)}, u32[]{:S(2)}, u32[]{:S(2)}) collective-permute-start(bf16[576,256]{1,0:T(8,128)(2,1)S(1)} %get-tuple-element.131), channel_id=1, source_target_pairs={{0,1},{1,2},{2,3},{3,0},{4,5},{5,6},{6,7},{7,4},{8,9},{9,10},{10,1... | collective-permute-start | bytes 884744 | tf_op jit(solution)/shard_map/ppermute | solution.py:400
  109.3 29.4 %collective-permute-start.38 = (bf16[768,256]{1,0:T(8,128)(2,1)S(1)}, bf16[768,256]{1,0:T(8,128)(2,1)S(1)}, u32[]{:S(2)}, u32[]{:S(2)}) collective-permute-start(bf16[768,256]{1,0:T(8,128)(2,1)S(1)} %get-tuple-element.136), channel_id=1, source_target_pairs={{0,12},{1,13},{2,14},{3,15},{4,0},{5,1},{6,2},{7,3},{8,4},{9,5},{1... | collective-permute-start | bytes 1179656 | tf_op jit(solution)/shard_map/ppermute | solution.py:400
  111.6 27.3 %collective-permute-start.39 = (bf16[768,256]{1,0:T(8,128)(2,1)S(1)}, bf16[768,256]{1,0:T(8,128)(2,1)S(1)}, u32[]{:S(2)}, u32[]{:S(2)}) collective-permute-start(bf16[768,256]{1,0:T(8,128)(2,1)S(1)} %get-tuple-element.137), channel_id=1, source_target_pairs={{0,3},{1,0},{2,1},{3,2},{4,7},{5,4},{6,5},{7,6},{8,11},{9,8},{10,9... | collective-permute-start | bytes 1179656 | tf_op jit(solution)/shard_map/ppermute | solution.py:400
  112.5 16.1 %collective-permute-start.27 = (bf16[576,256]{1,0:T(8,128)(2,1)S(1)}, bf16[576,256]{1,0:T(8,128)(2,1)S(1)}, u32[]{:S(2)}, u32[]{:S(2)}) collective-permute-start(bf16[576,256]{1,0:T(8,128)(2,1)S(1)} %get-tuple-element.124), channel_id=1, source_target_pairs={{0,12},{1,13},{2,14},{3,15},{4,0},{5,1},{6,2},{7,3},{8,4},{9,5},{1... | collective-permute-start | bytes 884744 | tf_op jit(solution)/shard_map/ppermute | solution.py:400
  118.7 19.8 %collective-permute-start.29 = (bf16[576,256]{1,0:T(8,128)(2,1)S(1)}, bf16[576,256]{1,0:T(8,128)(2,1)S(1)}, u32[]{:S(2)}, u32[]{:S(2)}) collective-permute-start(bf16[576,256]{1,0:T(8,128)(2,1)S(1)} %get-tuple-element.126), channel_id=1, source_target_pairs={{0,4},{1,5},{2,6},{3,7},{4,8},{5,9},{6,10},{7,11},{8,12},{9,13},{1... | collective-permute-start | bytes 884744 | tf_op jit(solution)/shard_map/ppermute | solution.py:400
  128.6 17.8 %collective-permute-start.41 = (bf16[768,256]{1,0:T(8,128)(2,1)S(1)}, bf16[768,256]{1,0:T(8,128)(2,1)S(1)}, u32[]{:S(2)}, u32[]{:S(2)}) collective-permute-start(bf16[768,256]{1,0:T(8,128)(2,1)S(1)} %get-tuple-element.139), channel_id=1, source_target_pairs={{0,1},{1,2},{2,3},{3,0},{4,5},{5,6},{6,7},{7,4},{8,9},{9,10},{10,1... | collective-permute-start | bytes 1179656 | tf_op jit(solution)/shard_map/ppermute | solution.py:400
  138.5 22.6 %collective-permute-start.46 = (bf16[768,256]{1,0:T(8,128)(2,1)S(1)}, bf16[768,256]{1,0:T(8,128)(2,1)S(1)}, u32[]{:S(2)}, u32[]{:S(2)}) collective-permute-start(bf16[768,256]{1,0:T(8,128)(2,1)S(1)} %get-tuple-element.148), channel_id=1, source_target_pairs={{0,8},{1,9},{2,10},{3,11},{4,12},{5,13},{6,14},{7,15},{8,0},{9,1},... | collective-permute-start | bytes 1179656 | tf_op jit(solution)/shard_map/ppermute | solution.py:400
  138.7 22.4 %collective-permute-start.47 = (bf16[768,256]{1,0:T(8,128)(2,1)S(1)}, bf16[768,256]{1,0:T(8,128)(2,1)S(1)}, u32[]{:S(2)}, u32[]{:S(2)}) collective-permute-start(bf16[768,256]{1,0:T(8,128)(2,1)S(1)} %get-tuple-element.149), channel_id=1, source_target_pairs={{0,2},{1,3},{2,0},{3,1},{4,6},{5,7},{6,4},{7,5},{8,10},{9,11},{10,... | collective-permute-start | bytes 1179656 | tf_op jit(solution)/shard_map/ppermute | solution.py:400
  138.8 22.4 %collective-permute-start.42 = (bf16[768,256]{1,0:T(8,128)(2,1)S(1)}, bf16[768,256]{1,0:T(8,128)(2,1)S(1)}, u32[]{:S(2)}, u32[]{:S(2)}) collective-permute-start(bf16[768,256]{1,0:T(8,128)(2,1)S(1)} %get-tuple-element.142), channel_id=1, source_target_pairs={{0,8},{1,9},{2,10},{3,11},{4,12},{5,13},{6,14},{7,15},{8,0},{9,1},... | collective-permute-start | bytes 1179656 | tf_op jit(solution)/shard_map/ppermute | solution.py:400
  142.5 23.9 %collective-permute-start.43 = (bf16[768,256]{1,0:T(8,128)(2,1)S(1)}, bf16[768,256]{1,0:T(8,128)(2,1)S(1)}, u32[]{:S(2)}, u32[]{:S(2)}) collective-permute-start(bf16[768,256]{1,0:T(8,128)(2,1)S(1)} %get-tuple-element.143), channel_id=1, source_target_pairs={{0,2},{1,3},{2,0},{3,1},{4,6},{5,7},{6,4},{7,5},{8,10},{9,11},{10,... | collective-permute-start | bytes 1179656 | tf_op jit(solution)/shard_map/ppermute | solution.py:400
  146.4 20.0 %collective-permute-start.44 = (bf16[768,256]{1,0:T(8,128)(2,1)S(1)}, bf16[768,256]{1,0:T(8,128)(2,1)S(1)}, u32[]{:S(2)}, u32[]{:S(2)}) collective-permute-start(bf16[768,256]{1,0:T(8,128)(2,1)S(1)} %get-tuple-element.144), channel_id=1, source_target_pairs={{0,12},{1,13},{2,14},{3,15},{4,0},{5,1},{6,2},{7,3},{8,4},{9,5},{1... | collective-permute-start | bytes 1179656 | tf_op jit(solution)/shard_map/ppermute | solution.py:400
  (22 other events, 277.3 us)
